TPU v7x, 256 devices: a whole 4x4x8 slice. The times are simulated.
256 devices in a mesh: tile: 64 (over z, x, core), mp: 4 (over y).
Axes of the slice: x: 4, y: 4, z: 8, core: 2. Of those that a mesh axis runs over, the one named last changes fastest.
Arguments:
- latent: bfloat16 [768, 384], P('tile'), may hold values from -19 to 19, as said below
- reward_grad: float32 [768, 384], P('tile'), may hold values from -6 to 6
- curvature: float32 [768, 384], P('tile'), may hold values from 0.3 to 3
- offsets: int32 [128, 2], P('tile'), may hold values from 0 to 736, as said below
- counts: int32 [768, 96], P('tile'), may hold values from 1 to 4, as said below
- w_in: bfloat16 [16, 640], replicated, may hold values from -3.2 to 3.2, as said below
- w_value: bfloat16 [640, 2560], P(None, 'mp'), may hold values from -0.25 to 0.25
- w_gate: bfloat16 [640, 2560], P(None, 'mp'), may hold values from -0.25 to 0.25
- w_down: bfloat16 [2560, 640], P('mp'), may hold values from -0.125 to 0.125
- w_out: bfloat16 [640, 16], replicated, may hold values from -0.25 to 0.25
Outputs:
- blended: float32 [768, 384], P('tile')
- grad_in: float32 [16, 640], replicated
- grad_value: float32 [640, 2560], P(None, 'mp')
- grad_gate: float32 [640, 2560], P(None, 'mp')
- grad_down: float32 [2560, 640], P('mp')
- grad_out: float32 [640, 16], replicated
Inputs may be any that keep to these rules, and one draw needn't show every extreme that they name: `offsets`: the corners are the points of a grid of 32 by 4 points spaced 24, each point taken by exactly one tile in a random order, each moved by at most 4 along each direction; the grid's first row and column stay at 0 and its last row and column are clamped to 736 and 64. The tiles cover every cell of the canvas. `counts`: the number of tiles whose 32 x 32 square holds the cell. `latent`: Real-valued. `w_in`: Real-valued.
All inputs are finite; a program needn't handle non-finite values.
Results may differ from a plain program's by a relative error of at most 0.003.
The roundings to bfloat16 on the way count: a program that leaves them out, or rounds other values in their place, can miss the bound.
Values may be sent and summed in bfloat16 or wider, within the bound.
A program may use at most 64 MiB of HBM per device.

v0:
```python
import math

import jax
import jax.numpy as jnp
from jax import lax
from jax.sharding import PartitionSpec as P

S = 32


layer_eps = 1e-05
root_half = 0.7071067811865476
inv_root_two_pi = 0.3989422804014327
highest = lax.Precision.HIGHEST


def gelu_value(inputs):
    return 0.5 * inputs * (1.0 + lax.erf(inputs * root_half))


def gelu_slope(inputs):
    return (
        0.5 * (1.0 + lax.erf(inputs * root_half))
        + inputs * jnp.exp(-0.5 * inputs * inputs) * inv_root_two_pi
    )


def patchify(cropped, channels):
    half_side = cropped.shape[0] // 2
    return (
        cropped.reshape(half_side, 2, half_side, 2 * channels)
        .transpose(0, 2, 1, 3)
        .reshape(half_side * half_side, 4 * channels)
    )


def unpatch(tokens, tile_side, channels):
    half_side = tile_side // 2
    token_rows = tokens.shape[0] // half_side
    return (
        tokens.reshape(token_rows, half_side, 2, 2 * channels)
        .transpose(0, 2, 1, 3)
        .reshape(2 * token_rows, tile_side * channels)
    )


def layer_norm(hidden):
    values = hidden.astype(jnp.float32)
    center = values - jnp.mean(values, axis=-1, keepdims=True)
    variance = jnp.mean(center * center, axis=-1, keepdims=True)
    inv_scale = lax.rsqrt(variance + layer_eps)
    return (center * inv_scale, inv_scale)


def norm_backward(normed, inv_scale, d_unit):
    centered = d_unit - jnp.mean(d_unit, axis=-1, keepdims=True)
    return inv_scale * (centered - normed * jnp.mean(d_unit * normed, axis=-1, keepdims=True))


def contract_rows(left, right):
    return lax.dot_general(
        left, right, (((0,), (0,)), ((), ())), preferred_element_type=jnp.float32
    )


def contract_rows_exact(left, right):
    return lax.dot_general(
        left, right, (((0,), (0,)), ((), ())), precision=highest, preferred_element_type=jnp.float32
    )


def contract_cols(left, right):
    return lax.dot_general(
        left, right, (((1,), (1,)), ((), ())), preferred_element_type=jnp.float32
    )


def crop_tiles(source, corners, tile_side, channels):

    def crop_one(corner):
        cropped = lax.dynamic_slice(
            source, (corner[0], corner[1] * channels), (tile_side, tile_side * channels)
        )
        return patchify(cropped, channels)

    return jax.vmap(crop_one)(corners)


def place_tiles(canvas, pieces, corners, row_shift, channels):
    piece_rows = pieces.shape[1]
    piece_cols = pieces.shape[2]

    def add_tile(tile_index, current):
        corner = corners[tile_index]
        start_row = corner[0] + row_shift
        start_col = corner[1] * channels
        existing = lax.dynamic_slice(current, (start_row, start_col), (piece_rows, piece_cols))
        return lax.dynamic_update_slice(
            current, existing + pieces[tile_index], (start_row, start_col)
        )

    return lax.fori_loop(0, pieces.shape[0], add_tile, canvas)


def per_device(
    latent, reward_grad, curvature, offsets, counts, w_in, w_value, w_gate, w_down, w_out
):
    channels = w_in.shape[0] // 4
    model_width = w_in.shape[1]
    tile_side = S
    half_side = tile_side // 2
    token_count = half_side * half_side
    tiles_here = offsets.shape[0]
    slab_rows = latent.shape[0]
    canvas_cols = latent.shape[1]
    tile_devices = lax.axis_size("tile")
    model_devices = lax.axis_size("mp")
    model_pos = lax.axis_index("mp")
    share_tokens = token_count // model_devices
    share_pixels = tile_side // model_devices
    scale_factor = 16.0 / math.sqrt(tiles_here * tile_devices * token_count)
    w_out_wide = w_out.astype(jnp.float32)
    cover_count = jnp.repeat(counts, channels, axis=1).astype(jnp.float32)
    placed_row = model_pos * share_pixels
    latent_source = lax.all_gather(latent, "tile", axis=0, tiled=True)
    patches = crop_tiles(latent_source, offsets, tile_side, channels)
    flat_patches = jnp.transpose(patches, (1, 0, 2)).reshape(token_count * tiles_here, 4 * channels)
    hidden = jnp.dot(flat_patches, w_in, preferred_element_type=jnp.float32).astype(jnp.bfloat16)
    normed, inv_scale = layer_norm(hidden)
    unit_in = normed.astype(jnp.bfloat16)
    value_proj = jnp.dot(unit_in, w_value, preferred_element_type=jnp.float32)
    gate_proj = jnp.dot(unit_in, w_gate, preferred_element_type=jnp.float32)
    active = (value_proj * gelu_value(gate_proj)).astype(jnp.bfloat16)
    active_grid = active.reshape(token_count, tiles_here, active.shape[1])

    def take_share(values):
        grid = values.reshape(token_count, tiles_here, values.shape[-1])
        picked = lax.dynamic_slice_in_dim(grid, model_pos * share_tokens, share_tokens, 0)
        return picked.reshape(share_tokens * tiles_here, values.shape[-1])

    hidden_share = take_share(hidden)
    row_block = active_grid.reshape(
        lax.axis_size("mp") * share_tokens * tiles_here, active_grid.shape[2]
    )
    ff_share = lax.psum_scatter(
        jnp.dot(row_block, w_down, preferred_element_type=jnp.float32).reshape(
            lax.axis_size("mp") * share_tokens, tiles_here, model_width
        ),
        "mp",
        scatter_dimension=0,
        tiled=True,
    ).reshape(share_tokens * tiles_here, model_width)
    noise_share = jnp.dot(hidden_share, w_out, preferred_element_type=jnp.float32) + jnp.dot(
        ff_share, w_out_wide, precision=highest, preferred_element_type=jnp.float32
    )
    noise_tiles = jnp.transpose(
        noise_share.reshape(share_tokens, tiles_here, w_out.shape[1]), (1, 0, 2)
    )

    def unpatch_share(tokens):
        return unpatch(tokens, tile_side, channels)

    noise_pieces = jax.vmap(unpatch_share)(noise_tiles)
    canvas_term = place_tiles(
        jnp.zeros((slab_rows * tile_devices, canvas_cols), jnp.float32),
        noise_pieces,
        offsets,
        placed_row,
        channels,
    )
    share_total = lax.psum_scatter(canvas_term, ("tile", "mp"), scatter_dimension=0, tiled=True)
    rows_each = slab_rows // model_devices
    first_share = model_pos * rows_each
    share_cover = lax.dynamic_slice_in_dim(cover_count, first_share, rows_each, 0)
    share_reward = lax.dynamic_slice_in_dim(reward_grad, first_share, rows_each, 0)
    share_curve = lax.dynamic_slice_in_dim(curvature, first_share, rows_each, 0)
    share_blend = share_total / share_cover
    share_cot = ((share_reward - share_curve * share_blend) / share_cover * scale_factor).astype(
        jnp.bfloat16
    )
    blended = lax.all_gather(share_blend, "mp", axis=0, tiled=True)
    cot_source = lax.all_gather(share_cot, ("tile", "mp"), axis=0, tiled=True)
    cot_patches = crop_tiles(cot_source, offsets, tile_side, channels)
    cot_flat = jnp.transpose(cot_patches, (1, 0, 2)).reshape(token_count * tiles_here, 4 * channels)
    cot_share = take_share(cot_flat)
    d_feat = contract_cols(cot_flat, w_out)
    d_feat_b = d_feat.astype(jnp.bfloat16)
    d_active = contract_cols(d_feat_b, w_down)
    down_term = contract_rows(active, d_feat_b)
    d_value = (d_active * gelu_value(gate_proj)).astype(jnp.bfloat16)
    d_gate = (d_active * value_proj * gelu_slope(gate_proj)).astype(jnp.bfloat16)
    value_term = contract_rows(unit_in, d_value)
    gate_term = contract_rows(unit_in, d_gate)
    d_value_grid = d_value.reshape(token_count, tiles_here, d_value.shape[1])
    d_gate_grid = d_gate.reshape(token_count, tiles_here, d_gate.shape[1])
    value_block = d_value_grid.reshape(
        share_tokens * lax.axis_size("mp") * tiles_here, d_value.shape[1]
    )
    gate_block = d_gate_grid.reshape(
        share_tokens * lax.axis_size("mp") * tiles_here, d_gate.shape[1]
    )
    summed = contract_cols(value_block, w_value) + contract_cols(gate_block, w_gate)
    d_unit_share = (
        lax.psum_scatter(
            summed.reshape(share_tokens * lax.axis_size("mp"), tiles_here, model_width).astype(
                jnp.bfloat16
            ),
            "mp",
            scatter_dimension=0,
            tiled=True,
        )
        .astype(jnp.float32)
        .reshape(share_tokens * tiles_here, model_width)
    )
    d_hidden = (
        take_share(d_feat) + norm_backward(take_share(normed), take_share(inv_scale), d_unit_share)
    ).astype(jnp.bfloat16)
    in_term = contract_rows(take_share(flat_patches), d_hidden)
    out_term = contract_rows(hidden_share, cot_share) + contract_rows_exact(
        ff_share, cot_share.astype(jnp.float32)
    )
    grad_in, grad_out = lax.psum((in_term, out_term), ("tile", "mp"))
    grad_value, grad_gate, grad_down = lax.psum((value_term, gate_term, down_term), "tile")
    return (blended, grad_in, grad_value, grad_gate, grad_down, grad_out)


def solution(mesh):
    return jax.shard_map(
        per_device,
        mesh=mesh,
        in_specs=(
            P("tile", None),
            P("tile", None),
            P("tile", None),
            P("tile", None),
            P("tile", None),
            P(),
            P(None, "mp"),
            P(None, "mp"),
            P("mp", None),
            P(),
        ),
        out_specs=(P("tile", None), P(), P(None, "mp"), P(None, "mp"), P("mp", None), P()),
        check_vma=False,
    )
```

profile of v0, /device:TPU:1, one launch (start us, length us, event | category | flops | bytes accessed | tf_op | source)
XLA Modules:
  0.0 970.5 jit_solution(10086862064302789510)
XLA Ops:
  7.2 0.8 compare_select_fusion.1
  8.1 55.0 %all-gather = bf16[64,12,384]{2,1,0:T(8,128)(2,1)S(1)} all-gather(bf16[1,12,384]{2,1,0:T(8,128)(2,1)} %bitcast.107), channel_id=1, replica_groups=mesh['tile'=64,'mp'=4] {'tile'}, dimensions={0}, use_global_device_ids=true | all-gather | bytes 599040 | tf_op jit(solution)/shard_map/all_gather | solution.py:125
  63.3 4.0 while.16
  63.3 0.6 fusion.74
  63.9 1.4 bitcast_dynamic-update-slice_fusion.4
  65.3 0.6 fusion.74
  65.9 1.4 bitcast_dynamic-update-slice_fusion.4
  68.9 0.8 fusion.39
  70.0 1.9 multiply_convert_fusion.1
  71.9 0.7 fusion.47
  72.7 1.8 reshape.143
  75.2 0.6 dynamic-slice.14
  76.7 47.1 %all-reduce.9.cloned.1.call-done = f32[256,2,640]{2,1,0:T(2,128)} async-done(((f32[256,2,640]{2,1,0:T(2,128)}), f32[256,2,640]{2,1,0:T(2,128)}) %all-reduce.9.cloned.1.call-update) | async-done | bytes 1310736
  123.8 1.0 constant_dynamic-slice_fusion.9
  126.0 5.4 while.15
  126.0 0.6 fusion.73
  128.0 0.6 dynamic_update_slice.8
  128.7 0.6 fusion.73
  130.7 0.6 dynamic_update_slice.8
  131.3 1.4 copy.70
  132.8 0.8 rsqrt.19
  133.7 0.8 constant_dynamic-slice_fusion.6
  134.8 1.3 fusion
  136.0 256.3 %all-reduce.11.cloned.1.call-done = f32[768,384]{0,1:T(8,128)} async-done(((f32[768,384]{0,1:T(8,128)}), f32[768,384]{0,1:T(8,128)}) %all-reduce.11.cloned.1.call-update) | async-done | bytes 1179664
  392.4 1.9 fusion.23
  394.4 75.3 %all-gather.2 = bf16[256,3,384]{2,1,0:T(4,128)(2,1)S(1)} all-gather(bf16[1,3,384]{2,1,0:T(4,128)(2,1)S(1)} %copy.75), channel_id=1, replica_groups=mesh['tile'=64,'mp'=4] {'tile','mp'}, dimensions={0}, use_global_device_ids=true | all-gather | bytes 592128 | tf_op jit(solution)/shard_map/all_gather | solution.py:182
  469.7 0.5 reshape.196
  470.2 4.0 while.17
  470.2 0.6 fusion.75
  470.8 1.4 bitcast_dynamic-update-slice_fusion.5
  472.2 0.6 fusion.75
  472.8 1.4 bitcast_dynamic-update-slice_fusion.5
  474.9 0.8 copy.77
  475.7 1.2 fusion.48
  476.9 2.9 fusion.9
  479.8 0.8 fusion.49
  480.8 0.5 copy-done.12
  481.4 1.6 fusion.2
  483.0 2.6 convert_element_type.57
  485.6 2.0 copy.80
  487.7 0.8 constant_dynamic-slice_fusion.4
  488.5 2.9 reshape.152
  491.5 1.7 constant_dynamic-slice_fusion.3
  493.2 1.8 reshape.151
  495.1 1.7 constant_dynamic-slice_fusion.5
  496.8 1.3 convolution_bitcast_fusion.1
  498.1 1.8 fusion.10
  499.9 3.1 fusion.35
  503.1 1.9 fusion.17
  504.9 2.5 reduce-scatter.3.cloned.1.call-done
  507.4 1.2 convert_reduce_fusion.1
  508.6 2.1 convolution_bitcast_fusion.2
  510.7 2.0 fusion.37
  512.8 0.9 copy-done.13
  513.8 9.1 all-gather.1
  522.9 0.6 reshape.194
  523.5 236.5 %all-reduce.13.cloned.1.call-done = (f32[16,640]{1,0:T(8,128)}, f32[640,16]{0,1:T(8,128)}) async-done(((f32[16,640]{1,0:T(8,128)}, f32[640,16]{0,1:T(8,128)}), (f32[16,640]{1,0:T(8,128)}, f32[640,16]{0,1:T(8,128)})) %all-reduce.13.cloned.1.call-update) | async-done | bytes 81936 | tf_op jit(solution)/shard_map/psum | solution.py:222
  760.0 195.9 %all-reduce.15.cloned.1.call-done = (f32[640,640]{1,0:T(8,128)}, f32[640,640]{1,0:T(8,128)}, f32[640,640]{1,0:T(8,128)}) async-done(((f32[640,640]{1,0:T(8,128)}, f32[640,640]{1,0:T(8,128)}, f32[640,640]{1,0:T(8,128)}), (f32[640,640]{1,0:T(8,128)}, f32[640,640]{1,0:T(8,128)}, f32[640,640]{1,0:T(8,128)})) %all-reduce.15.cloned.1.call-update) | async-done | bytes 4915216 | tf_op jit(solution)/shard_map/psum | solution.py:223
  955.9 1.4 copy.129
  957.3 2.8 copy.130
  960.1 1.2 copy.131
  961.3 0.9 copy-done.7
  962.2 1.2 copy.132
  963.3 0.6 copy.133
  (92 shorter events, 6.0 us)
Async XLA Ops:
  7.2 64.8 %copy-start = (bf16[640,640]{1,0:T(8,128)(2,1)S(1)}, bf16[640,640]{1,0:T(8,128)(2,1)}, u32[]{:S(2)}) copy-start(bf16[640,640]{1,0:T(8,128)(2,1)} %param.20) | copy-start | bytes 2457604
  7.2 116.6 %all-reduce.9.cloned.1.call-start = ((), (), s32[]{:S(2)}) async-start(), calls=%async_computation.2 | async-start | bytes 2621440
  63.1 5.0 copy-start.16
  63.3 5.6 copy-start.11
  68.9 1.1 copy-start.1
  70.0 1.9 copy-start.10
  74.5 0.7 copy-start.19
  74.5 2.0 copy-start.14
  74.6 317.8 %all-reduce.11.cloned.1.call-start = ((), (), s32[]{:S(2)}) async-start(), calls=%async_computation.3 | async-start | bytes 2359296
  75.0 1.7 copy-start.9
  124.8 1.0 copy-start.3
  124.8 1.1 copy-start.18
  131.3 2.3 copy-start.17
  132.7 374.7 %reduce-scatter.3.cloned.1.call-start = ((), (), s32[]{:S(2)}) async-start(), calls=%async_computation.1 | async-start | bytes 819200 | tf_op jit(solution)/shard_map/reduce_scatter | solution.py:204
  476.9 2.9 copy-start.2
  479.7 0.9 copy-start.4
  479.7 1.1 copy-start.6
  479.8 1.6 copy-start.12
  487.7 272.4 %all-reduce.13.cloned.1.call-start = ((), (), s32[]{:S(2)}) async-start(), calls=%async_computation.4 | async-start | bytes 163840 | tf_op jit(solution)/shard_map/psum | solution.py:222
  504.9 5.8 copy-start.5
  510.7 445.2 %all-reduce.15.cloned.1.call-start = ((), (), s32[]{:S(2)}) async-start(), calls=%async_computation.5 | async-start | bytes 9830400 | tf_op jit(solution)/shard_map/psum | solution.py:223
  512.8 0.9 copy-start.13
  957.3 2.8 copy-start.8
  960.1 2.0 copy-start.7
  962.2 1.2 copy-start.15
Sparse Core Ops, SparseCore 0:
  74.7 49.0 all-reduce.8
  132.9 259.4 all-reduce.10
  487.8 19.5 reduce-scatter.2
  513.5 246.4 all-reduce.12
  764.3 191.5 all-reduce.14
where the time goes:
time: 972 us; the launch traced here: 970 us
  waiting for transfers between devices  738 us (76%)
  blocking collectives  139 us (14%)
  local copies, waits for them, and re-layouts  46.1 us (5%)
  matrix products  22.9 us (2%)
  between operations  14.9 us (2%)
    unnamed x7, waiting for transfers between devices  304 us
    psum x1, waiting for transfers between devices, per_device(): grad_in, grad_out = lax.psum((in_term, out_term), ('tile', 'mp'))  237 us
    psum x1, waiting for transfers between devices, per_device(): lax.psum((value_term, gate_term, down_term), 'tile')  196 us
    all_gather x1, blocking collectives, per_device(): cot_source = lax.all_gather(share_cot, ('tile', 'mp'), axis=0, tiled=True)  75.3 us
    all_gather x1, blocking collectives, per_device(): latent_source = lax.all_gather(latent, 'tile', axis=0, tiled=True)  55 us
  transfers between devices with their start and end apart: 5, of which 5 were waited for; matrix products, arithmetic and copies ran while one was open for 3% of the time, Pallas kernels for 0%

commit v1 on v0

v1 whole, which is shorter than its diff:
```python
import functools
import math

import jax
import jax.numpy as jnp
from jax import lax
from jax.experimental import pallas as pl
from jax.experimental.pallas import tpu as pltpu
from jax.sharding import PartitionSpec as P

MESH = pl.DeviceIdType.MESH
bf16 = jnp.bfloat16
f32 = jnp.float32

SIDE = 32
HALF = 16
SPACING = 24
JITTER = 4
CH = 4
F = 16
D = 640
COLS = 384
CELLS = 96
SLAB = 12
REGION = 48
GRID_ROWS = 32
MP = 4
TILES = 128
layer_eps = 1e-05
root_half = 0.7071067811865476
inv_root_two_pi = 0.3989422804014327
SCALE = 16.0 / math.sqrt(TILES * HALF * HALF)
PAY = 2048


def dot(left, right, dims=((1,), (0,))):
    return lax.dot_general(left, right, (dims, ((), ())), preferred_element_type=f32)


NT = ((1,), (1,))
TN = ((0,), (0,))


def iota(shape, dim):
    return lax.broadcasted_iota(jnp.int32, shape, dim)


def one_hot(cond):
    return jnp.where(cond, 1.0, 0.0).astype(bf16)


def split3(x):
    hi = x.astype(bf16)
    rest = x - hi.astype(f32)
    mid = rest.astype(bf16)
    lo = (rest - mid.astype(f32)).astype(bf16)
    return hi, mid, lo


def split2(x):
    hi = x.astype(bf16)
    return hi, (x - hi.astype(f32)).astype(bf16)


def feature_of(lane):
    return (lane // 128) * 8 + lane % 8


def main_kernel(
    lat_h, rew_h, cur_h, cnt_h, win_h, wv_h, wg_h, wd_h, wo_h,
    blend_o, g_o, pin_o, pout_o,
    lat_s, cnt_s, rew_v, cur_v, win_v, wv, wg, wd, wo_v,
    regf, cntf, x_s, unit_s, hid_s, gel_s, vs_s, val_s, gate_s, act_s,
    part_s, rs_send, rs_in, cot_in, blend_in, cot_mine, blend_mine, wdo_s, woe_s,
    pay_s, pay_send, pay_in, z_in, z_mine, g_in, st_s, st_o, y_in, y_mine, p_in,
    loc_sem, send_sem, halo_sem, rs_sem, cot_sem, blend_sem, pay_sem, z_sem, g_sem, y_sem, p_sem,
):
    t = lax.axis_index("tile")
    p = lax.axis_index("mp")
    chip = t // 2
    k = t % 2
    up_chip = (chip + GRID_ROWS - 1) % GRID_ROWS
    down_chip = (chip + 1) % GRID_ROWS
    beside = jnp.where(k == 0, up_chip, down_chip)
    base8 = (t // 8) * 8
    member = t % 8
    plane = t // 8

    loads = []
    for n, (src, dst) in enumerate([
        (lat_h, lat_s.at[1 + k]), (cnt_h, cnt_s.at[1 + k]), (wd_h, wd), (wo_h, wo_v), (win_h, win_v),
        (wv_h, wv), (wg_h, wg), (rew_h, rew_v), (cur_h, cur_v),
    ]):
        copy = pltpu.make_async_copy(src, dst, loc_sem.at[n])
        copy.start()
        loads.append(copy)

    own_chip = [((2 * chip + (k + dk) % 2), (p + dq) % MP, (k + dk) % 2) for dk in range(2) for dq in range(MP)][1:]
    group = [(base8 + (member + n) % 8, (member + n) % 8) for n in range(1, 8)]
    planes = [(((plane + n) % 8) * 8 + member, (plane + n) % 8) for n in range(1, 8)]

    barrier = pltpu.get_barrier_semaphore()
    hellos = [(a, b) for a, b, _ in own_chip]
    hellos += [(2 * c + kk, q) for c in (up_chip, down_chip) for kk in range(2) for q in range(MP)]
    hellos += [(a, p) for a, _ in group] + [(a, p) for a, _ in planes]
    for target in hellos:
        pl.semaphore_signal(barrier, inc=1, device_id=target, device_id_type=MESH)
    pl.semaphore_wait(barrier, len(hellos))

    sent = []

    def send(src, dst, sem, target):
        copy = pltpu.make_async_remote_copy(
            src_ref=src, dst_ref=dst, send_sem=send_sem.at[len(sent)], recv_sem=sem,
            device_id=target, device_id_type=MESH,
        )
        copy.start()
        sent.append(copy)

    def arrive(dst, sem):
        pltpu.make_async_remote_copy(
            src_ref=dst, dst_ref=dst, send_sem=send_sem.at[0], recv_sem=sem,
            device_id=(t, p), device_id_type=MESH,
        ).wait_recv()

    far_slot = 3 * (1 - k)
    for target, slot in [((2 * chip + 1 - k, p), 1 + k), ((2 * beside, p), far_slot), ((2 * beside + 1, p), far_slot)]:
        send(lat_h, lat_s.at[slot], halo_sem.at[0, slot], target)
        send(cnt_h, cnt_s.at[slot], halo_sem.at[1, slot], target)

    lane256 = iota((1, 256), 1)
    expand = one_hot(iota((F, 256), 0) == feature_of(iota((F, 256), 1)))
    tj_mask = (iota((HALF, 1, 256), 2) % 128) // 8 == iota((HALF, 1, 256), 0)

    for copy in loads[2:5]:
        copy.wait()
    woe = dot(wo_v[...], expand).astype(bf16)
    woe_s[...] = woe
    wdo = dot(wd[...], woe)
    wdo_hi, wdo_lo = split2(wdo)
    wdo_s[0] = wdo_hi
    wdo_s[1] = wdo_lo
    win = win_v[...]
    wrep = dot(expand, win, TN).astype(bf16)

    loads[0].wait()
    loads[1].wait()
    for slot in (2 - k, 0, 3):
        arrive(lat_s.at[slot], halo_sem.at[0, slot])
        arrive(cnt_s.at[slot], halo_sem.at[1, slot])

    for slot in range(4):
        regf[SLAB * slot : SLAB * slot + SLAB, :] = lat_s[slot].astype(f32)
        cntf[SLAB * slot : SLAB * slot + SLAB, :] = cnt_s[slot].astype(f32)

    lane96 = iota((8, CELLS), 1)
    row_win = jnp.where(cntf[8:16, :] == 2.0, 1.0, 0.0)
    col_win = jnp.where(cntf[24:32, :] == 2.0, 1.0, 0.0)
    first_row = iota((8, CELLS), 0) == 0
    selects = []
    for j in range(2):
        c = 2 * k + j
        n_row = jnp.sum(jnp.where(lane96 == SPACING * c + 12, row_win, 0.0), axis=1, keepdims=True)
        n_row = jnp.sum(n_row, axis=0, keepdims=True)
        row = 16.0 - n_row
        row = jnp.where(chip == 0, 12.0, jnp.where(chip == GRID_ROWS - 1, 4.0, row))
        near = first_row & (lane96 >= SPACING * c - JITTER) & (lane96 < SPACING * c + JITTER)
        n_col = jnp.sum(jnp.where(near, col_win, 0.0), axis=1, keepdims=True)
        n_col = jnp.sum(n_col, axis=0, keepdims=True)
        col = (SPACING * c + JITTER).astype(f32) - n_col
        col = jnp.where(c == 0, 0.0, jnp.where(c == 3, float(CELLS - SIDE), col))
        m = iota((SIDE, REGION), 0)
        pick = (2 * (m % HALF) + m // HALF).astype(f32) + row
        sel_r = one_hot(iota((SIDE, REGION), 1).astype(f32) == pick)
        sel_c = one_hot(iota((COLS, 128), 0).astype(f32) == iota((COLS, 128), 1).astype(f32) + CH * col)
        m = iota((REGION, 3 * SIDE), 1) % SIDE
        pick = (2 * (m % HALF) + m // HALF).astype(f32) + row
        put_r = one_hot(iota((REGION, 3 * SIDE), 0).astype(f32) == pick)
        selects.append((sel_r, sel_c, put_r))

    def patches_of(region):
        tiles = []
        for sel_r, sel_c, _ in selects:
            rows = dot(sel_r, region).astype(bf16)
            crop = dot(rows, sel_c)
            pair = jnp.concatenate([crop[:HALF], crop[HALF:]], axis=1)
            full = jnp.where(tj_mask, pair.reshape(1, HALF, 256), 0.0)
            tiles.append(full.reshape(HALF * HALF, 256))
        return jnp.concatenate(tiles, axis=0)

    xf = patches_of(regf[...].astype(bf16))
    x = xf.astype(bf16)
    x_s[...] = x
    hidden = dot(x, wrep).astype(bf16)
    hid_s[...] = hidden
    values = hidden.astype(f32)
    center = values - jnp.mean(values, axis=-1, keepdims=True)
    variance = jnp.mean(center * center, axis=-1, keepdims=True)
    inv = lax.rsqrt(variance + layer_eps)
    unit = (center * inv).astype(bf16)
    unit_s[...] = unit

    loads[5].wait()
    loads[6].wait()
    value = dot(unit, wv[...])
    gate = dot(unit, wg[...])
    phi = 0.5 * (1.0 + lax.erf(gate * root_half))
    gel = gate * phi
    act = (value * gel).astype(bf16)
    act_s[...] = act
    gel_s[...] = gel
    val_s[...] = value
    gate_s[...] = gate
    vs_s[...] = value * (phi + gate * jnp.exp(-0.5 * gate * gate) * inv_root_two_pi)

    noise = dot(act, wdo_s[0]) + dot(act, wdo_s[1])
    own = dot(hid_s[...], woe_s[...])
    noise = noise + jnp.where(p == 0, own, 0.0)
    placed = None
    for j in range(2):
        block = noise[256 * j : 256 * j + 256].reshape(HALF, HALF, 256)
        crop = jnp.sum(jnp.where(tj_mask, block, 0.0), axis=0)
        stack = jnp.concatenate(
            [part[:, 128 * a : 128 * a + 128] for part in split3(crop) for a in range(2)], axis=0
        )
        wide = dot(stack, selects[j][1], NT).astype(bf16)
        term = dot(selects[j][2], wide)
        placed = term if placed is None else placed + term
    part_s[...] = placed
    for g in range(16):
        rs_send[g] = part_s[3 * g : 3 * g + 3, :]

    for dev, q, kk in own_chip:
        send(rs_send.at[4 + 4 * kk + q], rs_in.at[4 * k + p], rs_sem.at[4 * k + p], (dev, q))
    for q in range(MP):
        send(rs_send.at[q], rs_in.at[8 + 4 * k + p], rs_sem.at[8 + 4 * k + p], (2 * up_chip + 1, q))
        send(rs_send.at[12 + q], rs_in.at[8 + 4 * k + p], rs_sem.at[8 + 4 * k + p], (2 * down_chip, q))
    rs_in[4 * k + p] = rs_send[4 + 4 * k + p]

    xi = xf * inv
    xi_hi, xi_lo = split2(xi)
    pt = dot(expand, x, NT).astype(bf16)
    pit = jnp.concatenate([dot(expand, xi_hi, NT).astype(bf16), dot(expand, xi_lo, NT).astype(bf16)], axis=0)
    for copy in loads[7:9]:
        copy.wait()
    spread = one_hot(iota((CELLS, COLS), 0) == iota((CELLS, COLS), 1) // CH)
    cover = dot(cnt_s[1 + k].astype(f32).astype(bf16), spread)
    rew = rew_v[...]
    cur = cur_v[...]

    def my_rows(slab):
        out = slab[0:3]
        for q in range(1, MP):
            out = jnp.where(p == q, slab[3 * q : 3 * q + 3], out)
        return out

    cover3 = my_rows(cover)
    rew3 = my_rows(rew)
    cur3 = my_rows(cur)

    for dev, q, kk in own_chip:
        arrive(rs_in.at[4 * kk + q], rs_sem.at[4 * kk + q])
    for slot in range(8, 16):
        arrive(rs_in.at[slot], rs_sem.at[slot])
    total = rs_in[0]
    for slot in range(1, 16):
        total = total + rs_in[slot]
    blend3 = total / cover3
    cot3 = ((rew3 - cur3 * blend3) / cover3 * SCALE).astype(bf16).astype(f32)
    blend_mine[...] = blend3
    cot_mine[...] = cot3
    for dev, q, kk in own_chip:
        send(cot_mine, cot_in.at[4 + 4 * k + p], cot_sem.at[4 + 4 * k + p], (dev, q))
    slot = 12 * (1 - k) + p
    for kk in range(2):
        for q in range(MP):
            send(cot_mine, cot_in.at[slot], cot_sem.at[slot], (2 * beside + kk, q))
    for dq in range(1, MP):
        send(blend_mine, blend_in.at[p], blend_sem.at[p], (t, (p + dq) % MP))
    cot_in[4 + 4 * k + p] = cot3
    blend_in[p] = blend3

    for dev, q, kk in own_chip:
        arrive(cot_in.at[4 + 4 * kk + q], cot_sem.at[4 + 4 * kk + q])
    for q in range(MP):
        arrive(cot_in.at[q], cot_sem.at[q])
        arrive(cot_in.at[12 + q], cot_sem.at[12 + q])
    for g in range(16):
        regf[3 * g : 3 * g + 3, :] = cot_in[g]

    y = patches_of(regf[...].astype(bf16)).astype(bf16)
    dfb = dot(y, woe_s[...], NT).astype(bf16)
    d_act = dot(dfb, wd[...], NT)
    dv = (d_act * gel_s[...]).astype(bf16)
    dg = (d_act * vs_s[...]).astype(bf16)
    m2 = jnp.sum(dv.astype(f32) * val_s[...] + dg.astype(f32) * gate_s[...], axis=1, keepdims=True) * (1.0 / D)
    ct = dot(expand, y, NT).astype(bf16)
    gv = dot(pit, dv)
    gg = dot(pit, dg)
    gd = dot(ct, act_s[...])
    xm_hi, xm_lo = split2(xi * m2)
    b_w = dot(pit, xm_hi) + dot(pit, xm_lo)
    b_w = b_w[:F] + b_w[F:]
    a_w = dot(pt, y)
    at_w = dot(ct, x_s[...])

    def fold(wide):
        halves = []
        for a in range(2):
            part = wide[:, 128 * a : 128 * a + 128]
            for shift in (64, 32, 16, 8):
                part = part + pltpu.roll(part, shift, 1)
            halves.append(part)
        return halves

    lane128 = iota((F, 128), 1)
    small = jnp.zeros((F, 128), f32)
    for n, half in enumerate(fold(a_w) + fold(b_w) + fold(at_w)):
        small = jnp.where(lane128 // 8 == n, half, small)
    pay_s[:, 0:D] = gv[:F] + gv[F:]
    pay_s[:, D : 2 * D] = gg[:F] + gg[F:]
    pay_s[:, 2 * D : 3 * D] = gd
    pay_s[:, 3 * D : PAY] = small
    for c in range(8):
        pay_send[c] = pay_s[2 * c : 2 * c + 2, :]

    for dev, c in group:
        send(pay_send.at[c], pay_in.at[member], pay_sem.at[member], (dev, p))
    pay_in[member] = pay_send[member]
    for dev, c in group:
        arrive(pay_in.at[c], pay_sem.at[c])
    rows = pay_in[0]
    for c in range(1, 8):
        rows = rows + pay_in[c]
    z_mine[...] = rows
    for dev, c in planes:
        send(z_mine, z_in.at[plane], z_sem.at[plane], (dev, p))
    z_in[plane] = rows
    for dev, c in planes:
        arrive(z_in.at[c], z_sem.at[c])
    rows = z_in[0]
    for c in range(1, 8):
        rows = rows + z_in[c]
    g_in[member] = rows
    for dev, c in group:
        send(g_in.at[member], g_in.at[member], g_sem.at[member], (dev, p))

    def rows_dot(piece, right, dims):
        hi, mid, lo = split3(piece)
        width = piece.shape[1]
        st_s[0:2, 0:width] = hi.astype(f32)
        st_s[2:4, 0:width] = mid.astype(f32)
        st_s[4:6, 0:width] = lo.astype(f32)
        st_o[...] = dot(st_s[:, 0:width].astype(bf16), right, dims)
        return st_o[0:2, :] + st_o[2:4, :] + st_o[4:6, :]

    st_s[...] = jnp.zeros_like(st_s)
    small = rows[:, 3 * D : PAY]
    r16 = iota((128, F), 0)
    f16 = iota((128, F), 1)
    from_b = dot(one_hot(r16 == f16 + F), win).astype(bf16)
    from_t = dot(one_hot(r16 == f16 + 2 * F), win).astype(bf16)
    from_a = dot(one_hot(r16 == f16), wo_v[...], NT).astype(bf16)
    inner = rows_dot(rows[:, 0:D], wv[...], NT) + rows_dot(rows[:, D : 2 * D], wg[...], NT)
    inner = inner - rows_dot(small, from_b, ((1,), (0,)))
    inner = inner - jnp.mean(inner, axis=1, keepdims=True)
    y_mine[:, 0:D] = inner + 0.25 * rows_dot(small, from_a, ((1,), (0,)))
    outer = rows_dot(rows[:, 2 * D : 3 * D], wd[...], ((1,), (0,)))
    y_mine[:, D : 2 * D] = outer + 0.25 * rows_dot(small, from_t, ((1,), (0,)))
    y_in[p] = y_mine[...]
    for dq in range(1, MP):
        send(y_mine, y_in.at[p], y_sem.at[p], (t, (p + dq) % MP))
    for dq in range(1, MP):
        q = (p + dq) % MP
        arrive(y_in.at[q], y_sem.at[q])
    p_in[member] = y_in[0] + y_in[1] + y_in[2] + y_in[3]
    for dev, c in group:
        send(p_in.at[member], p_in.at[member], p_sem.at[member], (dev, p))

    for dq in range(1, MP):
        q = (p + dq) % MP
        arrive(blend_in.at[q], blend_sem.at[q])
    for q in range(MP):
        blend_o[3 * q : 3 * q + 3, :] = blend_in[q]
    for dev, c in group:
        arrive(g_in.at[c], g_sem.at[c])
    for c in range(8):
        g_o[2 * c : 2 * c + 2, :] = g_in[c][:, 0 : 3 * D]
    for dev, c in group:
        arrive(p_in.at[c], p_sem.at[c])
    for c in range(8):
        pin_o[2 * c : 2 * c + 2, :] = p_in[c][:, 0:D]
        pout_o[2 * c : 2 * c + 2, :] = p_in[c][:, D : 2 * D]
    for copy in sent:
        copy.wait_send()


def final_kernel(blend, g, pin, pout, win, wo, blend_o, gin_o, gv_o, gg_o, gd_o, gout_o):
    blend_o[...] = blend[...]
    gin_o[...] = pin[...]
    gout_o[...] = jnp.transpose(pout[...])
    w = win[...]
    w3 = jnp.concatenate([w, w, w], axis=0)
    mean = jnp.mean(w.astype(f32), axis=1, keepdims=True)
    eye = one_hot(iota((F, F), 0) == iota((F, F), 1))
    wot = dot(eye, wo[...], NT).astype(bf16)
    wot3 = jnp.concatenate([wot, wot, wot], axis=0)
    for n, out in enumerate((gv_o, gg_o)):
        rows = g[:, D * n : D * n + D]
        stack = jnp.concatenate(split3(rows), axis=0)
        out[...] = dot(w3, stack, TN) - jnp.sum(mean * rows, axis=0, keepdims=True)
    stack = jnp.concatenate(split3(g[:, 2 * D : 3 * D]), axis=0)
    gd_o[...] = dot(stack, wot3, TN)


def per_device(latent, reward_grad, curvature, offsets, counts, w_in, w_value, w_gate, w_down, w_out):
    vm = pltpu.VMEM
    any_spec = pl.BlockSpec(memory_space=pl.ANY)
    vm_spec = pl.BlockSpec(memory_space=pltpu.VMEM)
    tokens = 2 * HALF * HALF
    dma = pltpu.SemaphoreType.DMA
    scratch = [
        vm((4, SLAB, COLS), bf16), vm((4, SLAB, CELLS), jnp.int32), vm((SLAB, COLS), f32), vm((SLAB, COLS), f32),
        vm((F, D), bf16), vm((D, D), bf16), vm((D, D), bf16), vm((D, D), bf16), vm((D, F), bf16),
        vm((REGION, COLS), f32), vm((REGION, CELLS), f32), vm((tokens, 256), bf16), vm((tokens, D), bf16),
        vm((tokens, D), bf16), vm((tokens, D), f32), vm((tokens, D), f32), vm((tokens, D), f32), vm((tokens, D), f32),
        vm((tokens, D), bf16),
        vm((REGION, COLS), f32), vm((16, 3, COLS), f32), vm((16, 3, COLS), f32), vm((16, 3, COLS), f32),
        vm((MP, 3, COLS), f32), vm((3, COLS), f32), vm((3, COLS), f32), vm((2, D, 256), bf16), vm((D, 256), bf16),
        vm((F, PAY), f32), vm((8, 2, PAY), f32), vm((8, 2, PAY), f32), vm((8, 2, PAY), f32), vm((2, PAY), f32),
        vm((8, 2, PAY), f32), vm((8, D), f32), vm((8, D), f32), vm((MP, 2, 2 * D), f32), vm((2, 2 * D), f32),
        vm((8, 2, 2 * D), f32),
        dma((9,)), dma((70,)), dma((2, 4)), dma((16,)), dma((16,)), dma((MP,)), dma((8,)), dma((8,)), dma((8,)),
        dma((MP,)), dma((8,)),
    ]
    sds = jax.ShapeDtypeStruct
    blend, g, pin, pout = pl.pallas_call(
        main_kernel,
        out_shape=(sds((SLAB, COLS), f32), sds((F, 3 * D), f32), sds((F, D), f32), sds((F, D), f32)),
        in_specs=[any_spec] * 9,
        out_specs=(vm_spec,) * 4,
        scratch_shapes=scratch,
        compiler_params=pltpu.CompilerParams(
            collective_id=0, has_side_effects=True, vmem_limit_bytes=56 * 1024 * 1024
        ),
        name="tile_gradients",
    )(latent, reward_grad, curvature, counts, w_in, w_value, w_gate, w_down, w_out)
    return pl.pallas_call(
        final_kernel,
        out_shape=(
            sds((SLAB, COLS), f32), sds((F, D), f32), sds((D, D), f32), sds((D, D), f32), sds((D, D), f32),
            sds((D, F), f32),
        ),
        in_specs=[vm_spec] * 6,
        out_specs=(vm_spec,) * 6,
        name="weight_outputs",
    )(blend, g, pin, pout, w_in, w_out)


def solution(mesh):
    return jax.shard_map(
        per_device,
        mesh=mesh,
        in_specs=(
            P("tile", None), P("tile", None), P("tile", None), P("tile", None), P("tile", None), P(),
            P(None, "mp"), P(None, "mp"), P("mp", None), P(),
        ),
        out_specs=(P("tile", None), P(), P(None, "mp"), P(None, "mp"), P("mp", None), P()),
        check_vma=False,
    )
```

time: 972 us -> 59.4 us (0.06)
  waiting for transfers between devices: 738 us -> 0 us
  blocking collectives: 139 us -> 0 us
  Pallas kernels: 0 us -> 55.3 us
  local copies, waits for them, and re-layouts: 46.1 us -> 3.25 us
  matrix products: 22.9 us -> 0 us
  between operations: 14.9 us -> 0.64 us
    psum x2 -> x0, waiting for transfers between devices: 432 us -> none  [the longest x1 237 us: per_device(): grad_in, grad_out = lax.psum((in_term, out_term), ('tile', 'mp'))]
    unnamed x7 -> x0, waiting for transfers between devices: 304 us -> none
    all_gather x3 -> x0, blocking collectives: 139 us -> none  [the longest x1 75.3 us: per_device(): cot_source = lax.all_gather(share_cot, ('tile', 'mp'), axis=0, tiled=True)]
    pallas_call x0 -> x2, Pallas kernels: none -> 55.3 us  [the longest x1 51.1 us: per_device(): pl.pallas_call(main_kernel, out_shape=(sds((SLAB, COLS), f32), sds((F, 3...]
    dot_general x16 -> x0, matrix products: 22.9 us -> none  [the longest x5 10.9 us: contract_rows(): lax.dot_general(left, right, (((0,), (0,)), ((), ())), preferred_element_...]
    unnamed x56 -> x1, local copies, waits for them, and re-layouts: 13.6 us -> 1.53 us
  transfers between devices with their start and end apart: 5 -> 0, of which waited for: 5 -> 0; matrix products, arithmetic and copies ran while one was open for 3% -> 0% of each run, Pallas kernels for 0% -> 0%
where the time goes in v1:
time: 59.4 us; the launch traced here: 59.2 us
  Pallas kernels  55.3 us (93%)
  local copies, waits for them, and re-layouts  3.25 us (5%)
  between operations  0.64 us (1%)
    pallas_call x1, Pallas kernels, per_device(): pl.pallas_call(main_kernel, out_shape=(sds((SLAB, COLS), f32), sds((F, 3...  51.1 us
    pallas_call x1, Pallas kernels, per_device(): pl.pallas_call(final_kernel, out_shape=(sds((SLAB, COLS), f32), sds((F, D...  4.13 us
    pallas_call x1, local copies, waits for them, and re-layouts, per_device(): pl.pallas_call(final_kernel, out_shape=(sds((SLAB, COLS), f32), sds((F, D...  1.73 us
    unnamed x1, local copies, waits for them, and re-layouts  1.53 us

profile of v1, /device:TPU:1, one launch (start us, length us, event | category | flops | bytes accessed | tf_op | source)
XLA Modules:
  0.0 59.2 jit_solution(8383514921945143784)
XLA Ops:
  0.6 1.5 %copy.15.wo_h.wo = bf16[640,16]{1,0:T(8,128)(2,1)} copy(bf16[640,16]{0,1:T(8,128)(2,1)} %param.18) | data formatting | bytes 40960 | tf_op args[9]
  2.2 51.1 %tile_gradients.1 = (f32[12,384]{1,0:T(8,128)}, f32[16,1920]{1,0:T(8,128)}, f32[16,640]{1,0:T(8,128)}, f32[16,640]{1,0:T(8,128)}) custom-call(bf16[12,384]{1,0:T(8,128)(2,1)} %lat_h.1, f32[12,384]{1,0:T(8,128)} %rew_h.1, f32[12,384]{1,0:T(8,128)} %cur_h.1, s32[12,96]{1,0:T(8,128)} %cnt_h.1, bf16[16,640]{1,0:T(8,128)(2,1)} %win.1, bf16[640,640]{1,0:T(8,128)(2,1)} %wv_h.1, ...), custom_call_target="tpu_custom_call" | custom-call | tf_op jit(solution)/shard_map/tile_gradients/pallas_call | solution.py:437
  53.3 4.1 %weight_outputs.1 = (f32[12,384]{1,0:T(8,128)}, f32[16,640]{1,0:T(8,128)}, f32[640,640]{1,0:T(8,128)}, f32[640,640]{1,0:T(8,128)}, f32[640,640]{1,0:T(8,128)}, /*index=5*/f32[640,16]{1,0:T(8,128)}) custom-call(f32[12,384]{1,0:T(8,128)} %get-tuple-element.10.blend, f32[16,1920]{1,0:T(8,128)} %get-tuple-element.11.g, f32[16,640]{1,0:T(8,128)} %get-tuple-element.12.pin, ...), custom_call_target="tpu_custom_call" | custom-call | tf_op jit(solution)/shard_map/weight_outputs/pallas_call | solution.py:448
  57.4 1.7 %copy.17 = f32[640,16]{0,1:T(8,128)} copy(f32[640,16]{1,0:T(8,128)} %get-tuple-element.19) | data formatting | bytes 81920 | tf_op jit(solution)/shard_map/weight_outputs/pallas_call | solution.py:448

commit v2 on v1

v2 whole, which is shorter than its diff:
```python
import functools
import math

import jax
import jax.numpy as jnp
from jax import lax
from jax.experimental import pallas as pl
from jax.experimental.pallas import tpu as pltpu
from jax.sharding import PartitionSpec as P

MESH = pl.DeviceIdType.MESH
bf16 = jnp.bfloat16
f32 = jnp.float32

SIDE = 32
HALF = 16
SPACING = 24
JITTER = 4
CH = 4
F = 16
D = 640
COLS = 384
CELLS = 96
SLAB = 12
REGION = 48
GRID_ROWS = 32
MP = 4
TILES = 128
layer_eps = 1e-05
root_half = 0.7071067811865476
inv_root_two_pi = 0.3989422804014327
SCALE = 16.0 / math.sqrt(TILES * HALF * HALF)
PAY = 3 * D
LINK = f32
WIN = 256


def dot(left, right, dims=((1,), (0,))):
    return lax.dot_general(left, right, (dims, ((), ())), preferred_element_type=f32)


NT = ((1,), (1,))
TN = ((0,), (0,))


def iota(shape, dim):
    return lax.broadcasted_iota(jnp.int32, shape, dim)


def one_hot(cond):
    return jnp.where(cond, 1.0, 0.0).astype(bf16)


def split3(x):
    hi = x.astype(bf16)
    rest = x - hi.astype(f32)
    mid = rest.astype(bf16)
    lo = (rest - mid.astype(f32)).astype(bf16)
    return hi, mid, lo


def split2(x):
    hi = x.astype(bf16)
    return hi, (x - hi.astype(f32)).astype(bf16)


def feature_of(lane):
    return (lane // 128) * 8 + lane % 8


def main_kernel(
    lat_h, rew_h, cur_h, cnt_h, win_h, wv_h, wg_h, wd_h, wo_h,
    blend_o, g_o, p_o,
    lat_s, cnt_s, rew_v, cur_v, win_v, wv, wg, wd, wo_v,
    regf, cntf, x_s, hid_s, gel_s, vs_s, q_s, act_s,
    part_s, rs_send, rs_in, cot_in, blend_in, cot_mine, blend_mine, wdo_s, woe_s, wrep_s,
    pay_s, pay_send, pay_in, z_in, z_mine, g_in, ps_s, ps_send, ps_in, pz_in, pz_mine, p_in,
    lat_own, cnt_own, relay_sem, slab_sem,
    loc_sem, send_sem, halo_sem, rs_sem, cot_sem, blend_sem, pay_sem, z_sem, g_sem, ps_sem, pz_sem, p_sem,
):
    t = lax.axis_index("tile")
    p = lax.axis_index("mp")
    plane = t // 8
    member = t % 8
    base8 = plane * 8
    chip = t // 2
    k = t % 2
    across = t % 8 // 2
    odd = plane % 2

    def snake(row):
        z, r = row // 4, row % 4
        return 4 * z + jnp.where(z % 2 == 1, 3 - r, r)

    def shifted(row, n):
        return (row + n + GRID_ROWS) % GRID_ROWS

    grid_row = snake(chip)
    mirror = grid_row
    up_chip = snake(shifted(grid_row, -1))
    down_chip = snake(shifted(grid_row, 1))
    near_n = snake(shifted(chip, 2 * k - 1))
    beside = jnp.where(k == 0, up_chip, down_chip)
    in_place = odd == 0
    far_home = near_n == chip

    loads = []
    for n, (src, dst) in enumerate([
        (lat_h, lat_own), (cnt_h, cnt_own), (wd_h, wd), (wo_h, wo_v), (win_h, win_v), (wv_h, wv), (wg_h, wg),
    ]):
        copy = pltpu.make_async_copy(src, dst, loc_sem.at[n])
        copy.start()
        loads.append(copy)
    slab_loads = [pltpu.make_async_copy(rew_h, rew_v, loc_sem.at[7]), pltpu.make_async_copy(cur_h, cur_v, loc_sem.at[8])]

    @pl.when(in_place)
    def _():
        for copy in slab_loads:
            copy.start()

    own_chip = [((2 * chip + (k + dk) % 2), (p + dq) % MP, (k + dk) % 2) for dk in range(2) for dq in range(MP)][1:]
    group = [(base8 + (member + n) % 8, (member + n) % 8) for n in range(1, 8)]
    every = [
        (base8 + (member + n) % 8, (p + dq) % MP, ((member + n) % 8) * MP + (p + dq) % MP)
        for n in range(8) for dq in range(MP)
    ][1:]
    planes = [(((plane + n) % 8) * 8 + member, (plane + n) % 8) for n in range(1, 8)]

    def hello(sem, target):
        pl.semaphore_signal(sem, inc=1, device_id=target, device_id_type=MESH)

    sides = [(t, (p + 1) % MP), (t, (p + MP - 1) % MP)]
    levels = [(planes[0][0], p), (planes[6][0], p)]
    along = [(2 * up_chip + k, p), (2 * down_chip + k, p)]
    barrier = pltpu.get_barrier_semaphore()
    near = [(2 * mirror + 1 - k, p), (2 * near_n + 1 - k, p), (2 * mirror + 1 - k, p)]
    near += [(2 * chip + 1 - k, p)] + sides + levels + along
    near += [(2 * up_chip + 1 - k, p), (2 * down_chip + 1 - k, p)]
    for target in near:
        hello(barrier, target)
    maybe = [
        2 * mirror + k, 2 * near_n + k, 2 * mirror + k,
        2 * shifted(grid_row, -1) + 1, 2 * shifted(grid_row, 1),
    ]
    count = len(near)
    for target in maybe:
        @pl.when(target != t)
        def _():
            hello(barrier, (target, p))

        count = count + jnp.where(target != t, 1, 0)

    lane256 = iota((1, 256), 1)
    expand = one_hot(iota((F, 256), 0) == feature_of(iota((F, 256), 1)))
    tj_mask = (iota((HALF, 1, 256), 2) % 128) // 8 == iota((HALF, 1, 256), 0)

    for copy in loads[2:5]:
        copy.wait()
    woe = dot(wo_v[...], expand, TN).astype(bf16)
    woe_s[...] = woe
    wdo = dot(wd[...], woe)
    wdo_hi, wdo_lo = split2(wdo)
    wdo_s[0] = wdo_hi
    wdo_s[1] = wdo_lo
    win = win_v[...]
    wrep_s[...] = dot(expand, win, TN).astype(bf16)

    loads[0].wait()
    loads[1].wait()
    pl.semaphore_wait(barrier, count)
    sent = []

    def remote(src, dst, n, sem, target):
        return pltpu.make_async_remote_copy(
            src_ref=src, dst_ref=dst, send_sem=send_sem.at[n], recv_sem=sem,
            device_id=target, device_id_type=MESH,
        )

    def send(src, dst, sem, target):
        copy = remote(src, dst, len(sent), sem, target)
        copy.start()
        sent.append((None, copy))

    def send_if(cond, src, dst, sem, target):
        copy = remote(src, dst, len(sent), sem, target)

        @pl.when(cond)
        def _():
            copy.start()

        sent.append((cond, copy))

    def arrive(dst, sem):
        remote(dst, dst, 0, sem, (t, p)).wait_recv()

    far_slot = 3 * (1 - k)
    for chip_to, slot, home in ((near_n, far_slot, far_home), (mirror, 1 + k, in_place)):
        for n, (own, slots) in enumerate(((lat_own, lat_s), (cnt_own, cnt_s))):
            send(own, slots.at[slot], halo_sem.at[n, slot], (2 * chip_to + 1 - k, p))
            send_if(jnp.logical_not(home), own, slots.at[slot], halo_sem.at[n, slot], (2 * chip_to + k, p))

        @pl.when(home)
        def _():
            lat_s[slot] = lat_own[...]
            cnt_s[slot] = cnt_own[...]

    for n, (src, dst) in enumerate(((rew_h, rew_v), (cur_h, cur_v))):
        send_if(odd == 1, src, dst, slab_sem.at[n], (2 * mirror + k, p))

    def tell(step, targets):
        for target in targets:
            hello(relay_sem.at[step], target)

    def hear(step):
        pl.semaphore_wait(relay_sem.at[step], 2)

    tell(0, sides)
    tell(4, levels)

    def arrive_halo(slot):
        arrive(lat_s.at[slot], halo_sem.at[0, slot])
        arrive(cnt_s.at[slot], halo_sem.at[1, slot])

    arrive_halo(2 - k)
    for slot, remote_slot in (
        (1 + k, odd == 1),
        (0, 2 * shifted(grid_row, -1) + 1 != t),
        (3, 2 * shifted(grid_row, 1) != t),
    ):
        @pl.when(remote_slot)
        def _():
            arrive_halo(slot)

    hear(0)
    hear(4)
    tell(1, sides)
    tell(5, levels)

    for slot in range(4):
        slab = lat_s[slot].astype(f32)
        regf[SLAB * slot : SLAB * slot + SLAB, :] = jnp.where(k == 0, slab[:, 0:WIN], slab[:, COLS - WIN : COLS])
        cntf[SLAB * slot : SLAB * slot + SLAB, :] = cnt_s[slot].astype(f32)

    lane96 = iota((8, CELLS), 1)
    row_win = jnp.where(cntf[8:16, :] == 2.0, 1.0, 0.0)
    col_win = jnp.where(cntf[24:32, :] == 2.0, 1.0, 0.0)
    first_row = iota((8, CELLS), 0) == 0
    selects = []
    for j in range(2):
        c = 2 * k + j
        n_row = jnp.sum(jnp.where(lane96 == SPACING * c + 12, row_win, 0.0), axis=1, keepdims=True)
        n_row = jnp.sum(n_row, axis=0, keepdims=True)
        row = 16.0 - n_row
        row = jnp.where(grid_row == 0, 12.0, jnp.where(grid_row == GRID_ROWS - 1, 4.0, row))
        near = first_row & (lane96 >= SPACING * c - JITTER) & (lane96 < SPACING * c + JITTER)
        n_col = jnp.sum(jnp.where(near, col_win, 0.0), axis=1, keepdims=True)
        n_col = jnp.sum(n_col, axis=0, keepdims=True)
        col = (SPACING * c + JITTER).astype(f32) - n_col
        col = jnp.where(c == 0, 0.0, jnp.where(c == 3, float(CELLS - SIDE), col))
        m = iota((SIDE, REGION), 0)
        pick = (2 * (m % HALF) + m // HALF).astype(f32) + row
        sel_r = one_hot(iota((SIDE, REGION), 1).astype(f32) == pick)
        shift = CH * col - ((COLS - WIN) * k).astype(f32)
        sel_c = one_hot(iota((WIN, 128), 0).astype(f32) == iota((WIN, 128), 1).astype(f32) + shift)
        m = iota((REGION, 3 * SIDE), 1) % SIDE
        pick = (2 * (m % HALF) + m // HALF).astype(f32) + row
        put_r = one_hot(iota((REGION, 3 * SIDE), 0).astype(f32) == pick)
        selects.append((sel_r, sel_c, put_r))

    def patches_of(region):
        tiles = []
        for sel_r, sel_c, _ in selects:
            rows = dot(sel_r, region).astype(bf16)
            crop = dot(rows, sel_c)
            pair = jnp.concatenate([crop[:HALF], crop[HALF:]], axis=1)
            full = jnp.where(tj_mask, pair.reshape(1, HALF, 256), 0.0)
            tiles.append(full.reshape(HALF * HALF, 256))
        return jnp.concatenate(tiles, axis=0)

    xf = patches_of(regf[...].astype(bf16))
    x = xf.astype(bf16)
    x_s[...] = x
    hidden = dot(x, wrep_s[...]).astype(bf16)
    hid_s[...] = hidden
    values = hidden.astype(f32)
    center = values - jnp.mean(values, axis=-1, keepdims=True)
    variance = jnp.mean(center * center, axis=-1, keepdims=True)
    inv = lax.rsqrt(variance + layer_eps)
    unit = (center * inv).astype(bf16)

    loads[5].wait()
    loads[6].wait()
    value = dot(unit, wv[...])
    gate = dot(unit, wg[...])
    phi = 0.5 * (1.0 + lax.erf(gate * root_half))
    gel = gate * phi
    act = (value * gel).astype(bf16)
    act_s[...] = act
    gel_s[...] = gel
    slope = value * (phi + gate * jnp.exp(-0.5 * gate * gate) * inv_root_two_pi)
    vs_s[...] = slope
    q_s[...] = gel * value + slope * gate

    noise = dot(act, wdo_s[0]) + dot(act, wdo_s[1])
    own = dot(hid_s[...], woe_s[...])
    noise = noise + jnp.where(p == 0, own, 0.0)
    placed = None
    for j in range(2):
        block = noise[256 * j : 256 * j + 256].reshape(HALF, HALF, 256)
        crop = jnp.sum(jnp.where(tj_mask, block, 0.0), axis=0)
        stack = jnp.concatenate(
            [part[:, 128 * a : 128 * a + 128] for part in split3(crop) for a in range(2)], axis=0
        )
        wide = dot(stack, selects[j][1], NT).astype(bf16)
        term = dot(selects[j][2], wide)
        placed = term if placed is None else placed + term
    part_s[...] = placed
    for g in range(16):
        rs_send[g] = part_s[3 * g : 3 * g + 3, :]

    hear(1)
    hear(5)
    for dev, q, kk in own_chip:
        send(rs_send.at[4 + 4 * kk + q], rs_in.at[4 * k + p], rs_sem.at[4 * k + p], (dev, q))
    for q in range(MP):
        send(rs_send.at[q], rs_in.at[8 + 4 * k + p], rs_sem.at[8 + 4 * k + p], (2 * up_chip + 1, q))
        send(rs_send.at[12 + q], rs_in.at[8 + 4 * k + p], rs_sem.at[8 + 4 * k + p], (2 * down_chip, q))
    rs_in[4 * k + p] = rs_send[4 + 4 * k + p]

    tell(2, along)
    tell(6, levels)

    xi = xf * inv
    xi_hi, xi_lo = split2(xi)
    pt = dot(expand, x, NT).astype(bf16)
    pit = jnp.concatenate([dot(expand, xi_hi, NT).astype(bf16), dot(expand, xi_lo, NT).astype(bf16)], axis=0)

    @pl.when(in_place)
    def _():
        for copy in slab_loads:
            copy.wait()

    @pl.when(odd == 1)
    def _():
        arrive(rew_v, slab_sem.at[0])
        arrive(cur_v, slab_sem.at[1])

    spread = one_hot(iota((CELLS, COLS), 0) == iota((CELLS, COLS), 1) // CH)
    cover = dot(cnt_s[1 + k].astype(f32).astype(bf16), spread)
    rew = rew_v[...]
    cur = cur_v[...]

    def my_rows(slab):
        out = slab[0:3]
        for q in range(1, MP):
            out = jnp.where(p == q, slab[3 * q : 3 * q + 3], out)
        return out

    cover3 = my_rows(cover)
    rew3 = my_rows(rew)
    cur3 = my_rows(cur)

    for dev, q, kk in own_chip:
        arrive(rs_in.at[4 * kk + q], rs_sem.at[4 * kk + q])
    for slot in range(8, 16):
        arrive(rs_in.at[slot], rs_sem.at[slot])
    sums = []
    for kk in range(2):
        part = rs_in[4 * kk]
        for slot in [4 * kk + 1, 4 * kk + 2, 4 * kk + 3] + [8 + 4 * kk + q for q in range(MP)]:
            part = part + rs_in[slot]
        sums.append(part)
    left, right = sums
    total = jnp.concatenate([left[:, 0:128], left[:, 128:] + right[:, 0:128], right[:, 128:]], axis=1)
    blend3 = total / cover3
    cot3 = ((rew3 - cur3 * blend3) / cover3 * SCALE).astype(bf16).astype(f32)
    blend_mine[...] = blend3
    cot_mine[0] = cot3[:, 0:WIN]
    cot_mine[1] = cot3[:, COLS - WIN : COLS]
    for dev, q, kk in own_chip:
        send(cot_mine.at[kk], cot_in.at[4 + 4 * k + p], cot_sem.at[4 + 4 * k + p], (dev, q))
    slot = 12 * (1 - k) + p
    for kk in range(2):
        for q in range(MP):
            send(cot_mine.at[kk], cot_in.at[slot], cot_sem.at[slot], (2 * beside + kk, q))
    hear(2)
    hear(6)
    tell(3, along)
    cot_in[4 + 4 * k + p] = cot_mine[k]

    for dev, q, kk in own_chip:
        arrive(cot_in.at[4 + 4 * kk + q], cot_sem.at[4 + 4 * kk + q])
    for q in range(MP):
        arrive(cot_in.at[q], cot_sem.at[q])
        arrive(cot_in.at[12 + q], cot_sem.at[12 + q])
    hear(3)
    for dq in range(1, MP):
        send(blend_mine, blend_in.at[p], blend_sem.at[p], (2 * mirror + k, (p + dq) % MP))
    send_if(odd == 1, blend_mine, blend_in.at[p], blend_sem.at[p], (2 * mirror + k, p))

    @pl.when(in_place)
    def _():
        blend_in[p] = blend_mine[...]

    for g in range(16):
        regf[3 * g : 3 * g + 3, :] = cot_in[g]

    y = patches_of(regf[...].astype(bf16)).astype(bf16)
    dfb = dot(y, woe_s[...], NT).astype(bf16)
    d_act = dot(dfb, wd[...], NT)
    dv = (d_act * gel_s[...]).astype(bf16)
    dg = (d_act * vs_s[...]).astype(bf16)
    ct = dot(expand, y, NT).astype(bf16)
    gv = dot(pit, dv)
    gg = dot(pit, dg)
    gv = gv[:F] + gv[F:]
    gg = gg[:F] + gg[F:]
    gd = dot(ct, act_s[...])
    pay_s[:, 0:D] = gv
    pay_s[:, D : 2 * D] = gg
    pay_s[:, 2 * D : 3 * D] = gd
    for c in range(8):
        pay_send[c] = pay_s[2 * c : 2 * c + 2, :].astype(pay_send.dtype)

    for dev, c in group:
        send(pay_send.at[c], pay_in.at[member], pay_sem.at[member], (dev, p))
    pay_in[member] = pay_send[member]

    def rows_dot(piece, right, dims=((1,), (0,))):
        both = dot(jnp.concatenate(split2(piece), axis=0), right, dims)
        return both[:F] + both[F:]

    m2 = jnp.sum(d_act * q_s[...], axis=1, keepdims=True) * (1.0 / D)
    xm_hi, xm_lo = split2(xi * m2)
    b_w = dot(pit, xm_hi) + dot(pit, xm_lo)
    b_w = b_w[:F] + b_w[F:]
    inner = rows_dot(gv, wv[...], NT) + rows_dot(gg, wg[...], NT) - rows_dot(b_w, wrep_s[...])
    inner = inner - jnp.mean(inner, axis=1, keepdims=True)
    ps_s[0:F, :] = inner + 0.25 * rows_dot(dot(pt, y), woe_s[...], NT)
    ps_s[F : 2 * F, :] = rows_dot(gd, wd[...]) + 0.25 * rows_dot(dot(ct, x_s[...]), wrep_s[...])
    for n in range(2 * F):
        ps_send[n] = ps_s[n : n + 1, :]
    mine = MP * member + p
    for dev, q, n in every:
        send(ps_send.at[n], ps_in.at[mine], ps_sem.at[mine], (dev, q))
    ps_in[mine] = ps_send[mine]

    for dev, c in group:
        arrive(pay_in.at[c], pay_sem.at[c])
    rows = pay_in[0].astype(f32)
    for c in range(1, 8):
        rows = rows + pay_in[c].astype(f32)
    z_mine[...] = rows.astype(z_mine.dtype)
    for dev, c in planes:
        send(z_mine, z_in.at[plane], z_sem.at[plane], (dev, p))
    z_in[plane] = z_mine[...]

    for dev, q, n in every:
        arrive(ps_in.at[n], ps_sem.at[n])
    row = ps_in[0]
    for n in range(1, 2 * F):
        row = row + ps_in[n]
    pz_mine[...] = row
    for dev, c in planes:
        send(pz_mine, pz_in.at[plane], pz_sem.at[plane], (dev, p))
    pz_in[plane] = row

    for dev, c in planes:
        arrive(z_in.at[c], z_sem.at[c])
    rows = z_in[0].astype(f32)
    for c in range(1, 8):
        rows = rows + z_in[c].astype(f32)
    g_in[member] = rows
    for dev, c in group:
        send(g_in.at[member], g_in.at[member], g_sem.at[member], (dev, p))

    for dev, c in planes:
        arrive(pz_in.at[c], pz_sem.at[c])
    row = pz_in[0]
    for c in range(1, 8):
        row = row + pz_in[c]
    p_in[mine] = row
    for dev, q, n in every:
        send(p_in.at[mine], p_in.at[mine], p_sem.at[mine], (dev, q))

    for dq in range(1, MP):
        q = (p + dq) % MP
        arrive(blend_in.at[q], blend_sem.at[q])

    @pl.when(odd == 1)
    def _():
        arrive(blend_in.at[p], blend_sem.at[p])

    for q in range(MP):
        blend_o[3 * q : 3 * q + 3, :] = blend_in[q]
    for dev, c in group:
        arrive(g_in.at[c], g_sem.at[c])
    for c in range(8):
        g_o[2 * c : 2 * c + 2, :] = g_in[c]
    for dev, q, n in every:
        arrive(p_in.at[n], p_sem.at[n])
    for n in range(2 * F):
        p_o[n : n + 1, :] = p_in[n]
    for cond, copy in sent:
        if cond is None:
            copy.wait_send()
        else:
            pl.when(cond)(copy.wait_send)

def final_kernel(blend, g, both, win, wo, blend_o, gin_o, gv_o, gg_o, gd_o, gout_o, out_s, out_sem):
    w = win[...]
    w3 = jnp.concatenate([w, w, w], axis=0)
    mean = jnp.mean(w.astype(f32), axis=1, keepdims=True)
    wot = wo[...]
    wot3 = jnp.concatenate([wot, wot, wot], axis=0)
    half = D // 2
    copies = []
    for n, out in enumerate((gv_o, gg_o, gd_o)):
        rows = g[:, D * n : D * n + D]
        stack = jnp.concatenate(split3(rows), axis=0)
        left, right = (w3, stack) if n < 2 else (stack, wot3)
        for h in range(2):
            block = dot(left[:, half * h : half * h + half], right, TN)
            if n < 2:
                block = block - jnp.sum(mean * rows, axis=0, keepdims=True)
            out_s[n, half * h : half * h + half, :] = block
            copy = pltpu.make_async_copy(
                out_s.at[n, pl.ds(half * h, half)], out.at[pl.ds(half * h, half)], out_sem.at[2 * n + h]
            )
            copy.start()
            copies.append(copy)
    blend_o[...] = blend[...]
    gin_o[...] = both[0:F, :]
    gout_o[...] = both[F : 2 * F, :]
    for copy in copies:
        copy.wait()


def per_device(latent, reward_grad, curvature, offsets, counts, w_in, w_value, w_gate, w_down, w_out):
    vm = pltpu.VMEM
    any_spec = pl.BlockSpec(memory_space=pl.ANY)
    vm_spec = pl.BlockSpec(memory_space=pltpu.VMEM)
    tokens = 2 * HALF * HALF
    dma = pltpu.SemaphoreType.DMA
    scratch = [
        vm((4, SLAB, COLS), bf16), vm((4, SLAB, CELLS), jnp.int32), vm((SLAB, COLS), f32), vm((SLAB, COLS), f32),
        vm((F, D), bf16), vm((D, D), bf16), vm((D, D), bf16), vm((D, D), bf16), vm((F, D), bf16),
        vm((REGION, WIN), f32), vm((REGION, CELLS), f32), vm((tokens, 256), bf16), vm((tokens, D), bf16),
        vm((tokens, D), f32), vm((tokens, D), f32), vm((tokens, D), f32), vm((tokens, D), bf16),
        vm((REGION, WIN), f32), vm((16, 3, WIN), f32), vm((16, 3, WIN), f32), vm((16, 3, WIN), f32),
        vm((MP, 3, COLS), f32), vm((2, 3, WIN), f32), vm((3, COLS), f32), vm((2, D, 256), bf16), vm((D, 256), bf16),
        vm((256, D), bf16),
        vm((F, PAY), f32), vm((8, 2, PAY), LINK), vm((8, 2, PAY), LINK), vm((8, 2, PAY), LINK), vm((2, PAY), LINK),
        vm((8, 2, PAY), f32), vm((2 * F, D), f32), vm((2 * F, 1, D), f32), vm((2 * F, 1, D), f32), vm((8, 1, D), f32),
        vm((1, D), f32), vm((2 * F, 1, D), f32),
        vm((SLAB, COLS), bf16), vm((SLAB, CELLS), jnp.int32), pltpu.SemaphoreType.REGULAR((7,)), dma((2,)),
        dma((9,)), dma((136,)), dma((2, 4)), dma((16,)), dma((16,)), dma((MP,)), dma((8,)), dma((8,)), dma((8,)),
        dma((2 * F,)), dma((8,)), dma((2 * F,)),
    ]
    sds = jax.ShapeDtypeStruct
    blend, g, both = pl.pallas_call(
        main_kernel,
        out_shape=(sds((SLAB, COLS), f32), sds((F, 3 * D), f32), sds((2 * F, D), f32)),
        in_specs=[any_spec] * 9,
        out_specs=(vm_spec,) * 3,
        scratch_shapes=scratch,
        compiler_params=pltpu.CompilerParams(
            collective_id=0, has_side_effects=True, vmem_limit_bytes=56 * 1024 * 1024
        ),
        name="tile_gradients",
    )(latent, reward_grad, curvature, counts, w_in, w_value, w_gate, w_down, w_out.T)
    *outs, grad_out = pl.pallas_call(
        final_kernel,
        out_shape=(
            sds((SLAB, COLS), f32), sds((F, D), f32), sds((D, D), f32), sds((D, D), f32), sds((D, D), f32),
            sds((F, D), f32),
        ),
        in_specs=[vm_spec] * 5,
        out_specs=(vm_spec, vm_spec, any_spec, any_spec, any_spec, vm_spec),
        scratch_shapes=[vm((3, D, D), f32), dma((6,))],
        name="weight_outputs",
    )(blend, g, both, w_in, w_out.T)
    return (*outs, grad_out.T)


def solution(mesh):
    return jax.shard_map(
        per_device,
        mesh=mesh,
        in_specs=(
            P("tile", None), P("tile", None), P("tile", None), P("tile", None), P("tile", None), P(),
            P(None, "mp"), P(None, "mp"), P("mp", None), P(),
        ),
        out_specs=(P("tile", None), P(), P(None, "mp"), P(None, "mp"), P("mp", None), P()),
        check_vma=False,
    )
```

time: 59.4 us -> 52 us (0.88)
  Pallas kernels: 55.3 us -> 51.2 us
  local copies, waits for them, and re-layouts: 3.25 us -> 0 us
    pallas_call x1, Pallas kernels: 51.1 us -> 46.9 us  [per_device(): pl.pallas_call(main_kernel, out_shape=(sds((SLAB, COLS), f32), sds((F, 3...]
    pallas_call x1 -> x0, local copies, waits for them, and re-layouts: 1.73 us -> none  [per_device(): pl.pallas_call(final_kernel, out_shape=(sds((SLAB, COLS), f32), sds((F, D...]
    unnamed x1 -> x0, local copies, waits for them, and re-layouts: 1.53 us -> none
where the time goes in v2:
time: 52 us; the launch traced here: 51.9 us
  Pallas kernels  51.2 us (98%)
  between operations  0.64 us (1%)
    pallas_call x1, Pallas kernels, per_device(): pl.pallas_call(main_kernel, out_shape=(sds((SLAB, COLS), f32), sds((F, 3...  46.9 us
    pallas_call x1, Pallas kernels, per_device(): pl.pallas_call(final_kernel, out_shape=(sds((SLAB, COLS), f32), sds((F, D...  4.34 us

profile of v2, /device:TPU:1, one launch (start us, length us, event | category | flops | bytes accessed | tf_op | source)
XLA Modules:
  0.0 51.9 jit_solution(12084616132418113737)
XLA Ops:
  0.6 46.9 %tile_gradients.1 = (f32[12,384]{1,0:T(8,128)}, f32[16,1920]{1,0:T(8,128)}, f32[32,640]{1,0:T(8,128)}) custom-call(bf16[12,384]{1,0:T(8,128)(2,1)} %lat_h.1, f32[12,384]{1,0:T(8,128)} %rew_h.1, f32[12,384]{1,0:T(8,128)} %cur_h.1, s32[12,96]{1,0:T(8,128)} %cnt_h.1, bf16[16,640]{1,0:T(8,128)(2,1)} %win.1, bf16[640,640]{1,0:T(8,128)(2,1)} %wv_h.1, ...), custom_call_target="tpu_custom_call" | custom-call | tf_op jit(solution)/shard_map/tile_gradients/pallas_call | solution.py:561
  47.5 4.3 %weight_outputs.1 = (f32[12,384]{1,0:T(8,128)}, f32[16,640]{1,0:T(8,128)}, f32[640,640]{1,0:T(8,128)}, f32[640,640]{1,0:T(8,128)}, f32[640,640]{1,0:T(8,128)}, /*index=5*/f32[16,640]{1,0:T(8,128)}) custom-call(f32[12,384]{1,0:T(8,128)} %get-tuple-element.15.blend, f32[16,1920]{1,0:T(8,128)} %get-tuple-element.16.g, f32[32,640]{1,0:T(8,128)} %get-tuple-element.17.both, ...), custom_call_target="tpu_custom_call" | custom-call | tf_op jit(solution)/shard_map/weight_outputs/pallas_call | solution.py:572

commit v3 on v2

--- a/solution.py
+++ b/solution.py
@@ -31,7 +31,7 @@
 inv_root_two_pi = 0.3989422804014327
 SCALE = 16.0 / math.sqrt(TILES * HALF * HALF)
 PAY = 3 * D
-LINK = f32
+LINK = bf16
 WIN = 256
 
 
@@ -150,6 +150,58 @@
 
         count = count + jnp.where(target != t, 1, 0)
 
+    loads[0].wait()
+    loads[1].wait()
+    pl.semaphore_wait(barrier, count)
+    sent = []
+
+    def remote(src, dst, n, sem, target):
+        return pltpu.make_async_remote_copy(
+            src_ref=src, dst_ref=dst, send_sem=send_sem.at[n], recv_sem=sem,
+            device_id=target, device_id_type=MESH,
+        )
+
+    def send(src, dst, sem, target):
+        copy = remote(src, dst, len(sent), sem, target)
+        copy.start()
+        sent.append((None, copy))
+
+    def send_if(cond, src, dst, sem, target):
+        copy = remote(src, dst, len(sent), sem, target)
+
+        @pl.when(cond)
+        def _():
+            copy.start()
+
+        sent.append((cond, copy))
+
+    def arrive(dst, sem):
+        remote(dst, dst, 0, sem, (t, p)).wait_recv()
+
+    far_slot = 3 * (1 - k)
+    for chip_to, slot, home in ((near_n, far_slot, far_home), (mirror, 1 + k, in_place)):
+        for n, (own, slots) in enumerate(((lat_own, lat_s), (cnt_own, cnt_s))):
+            send(own, slots.at[slot], halo_sem.at[n, slot], (2 * chip_to + 1 - k, p))
+            send_if(jnp.logical_not(home), own, slots.at[slot], halo_sem.at[n, slot], (2 * chip_to + k, p))
+
+        @pl.when(home)
+        def _():
+            lat_s[slot] = lat_own[...]
+            cnt_s[slot] = cnt_own[...]
+
+    for n, (src, dst) in enumerate(((rew_h, rew_v), (cur_h, cur_v))):
+        send_if(odd == 1, src, dst, slab_sem.at[n], (2 * mirror + k, p))
+
+    def tell(step, targets):
+        for target in targets:
+            hello(relay_sem.at[step], target)
+
+    def hear(step):
+        pl.semaphore_wait(relay_sem.at[step], 2)
+
+    tell(0, sides)
+    tell(4, levels)
+
     lane256 = iota((1, 256), 1)
     expand = one_hot(iota((F, 256), 0) == feature_of(iota((F, 256), 1)))
     tj_mask = (iota((HALF, 1, 256), 2) % 128) // 8 == iota((HALF, 1, 256), 0)
@@ -164,58 +216,6 @@
     wdo_s[1] = wdo_lo
     win = win_v[...]
     wrep_s[...] = dot(expand, win, TN).astype(bf16)
-
-    loads[0].wait()
-    loads[1].wait()
-    pl.semaphore_wait(barrier, count)
-    sent = []
-
-    def remote(src, dst, n, sem, target):
-        return pltpu.make_async_remote_copy(
-            src_ref=src, dst_ref=dst, send_sem=send_sem.at[n], recv_sem=sem,
-            device_id=target, device_id_type=MESH,
-        )
-
-    def send(src, dst, sem, target):
-        copy = remote(src, dst, len(sent), sem, target)
-        copy.start()
-        sent.append((None, copy))
-
-    def send_if(cond, src, dst, sem, target):
-        copy = remote(src, dst, len(sent), sem, target)
-
-        @pl.when(cond)
-        def _():
-            copy.start()
-
-        sent.append((cond, copy))
-
-    def arrive(dst, sem):
-        remote(dst, dst, 0, sem, (t, p)).wait_recv()
-
-    far_slot = 3 * (1 - k)
-    for chip_to, slot, home in ((near_n, far_slot, far_home), (mirror, 1 + k, in_place)):
-        for n, (own, slots) in enumerate(((lat_own, lat_s), (cnt_own, cnt_s))):
-            send(own, slots.at[slot], halo_sem.at[n, slot], (2 * chip_to + 1 - k, p))
-            send_if(jnp.logical_not(home), own, slots.at[slot], halo_sem.at[n, slot], (2 * chip_to + k, p))
-
-        @pl.when(home)
-        def _():
-            lat_s[slot] = lat_own[...]
-            cnt_s[slot] = cnt_own[...]
-
-    for n, (src, dst) in enumerate(((rew_h, rew_v), (cur_h, cur_v))):
-        send_if(odd == 1, src, dst, slab_sem.at[n], (2 * mirror + k, p))
-
-    def tell(step, targets):
-        for target in targets:
-            hello(relay_sem.at[step], target)
-
-    def hear(step):
-        pl.semaphore_wait(relay_sem.at[step], 2)
-
-    tell(0, sides)
-    tell(4, levels)
 
     def arrive_halo(slot):
         arrive(lat_s.at[slot], halo_sem.at[0, slot])
@@ -491,30 +491,52 @@
     def _():
         arrive(blend_in.at[p], blend_sem.at[p])
 
-    for q in range(MP):
-        blend_o[3 * q : 3 * q + 3, :] = blend_in[q]
+    outs = [(blend_in, blend_o), (g_in, g_o), (p_in, p_o)]
+    outs = [pltpu.make_async_copy(src, dst, loc_sem.at[9 + n]) for n, (src, dst) in enumerate(outs)]
+    outs[0].start()
     for dev, c in group:
         arrive(g_in.at[c], g_sem.at[c])
-    for c in range(8):
-        g_o[2 * c : 2 * c + 2, :] = g_in[c]
+    outs[1].start()
     for dev, q, n in every:
         arrive(p_in.at[n], p_sem.at[n])
-    for n in range(2 * F):
-        p_o[n : n + 1, :] = p_in[n]
+    outs[2].start()
     for cond, copy in sent:
         if cond is None:
             copy.wait_send()
         else:
             pl.when(cond)(copy.wait_send)
-
-def final_kernel(blend, g, both, win, wo, blend_o, gin_o, gv_o, gg_o, gd_o, gout_o, out_s, out_sem):
-    w = win[...]
+    for copy in outs:
+        copy.wait()
+
+def final_kernel(
+    blend_h, g_h, both_h, win_h, wo_h, blend_o, gin_o, gv_o, gg_o, gd_o, gout_o,
+    blend_v, g_v, both_v, win_v, wo_v, g, blend_s, both_s, out_s, in_sem, out_sem,
+):
+    loads = [
+        pltpu.make_async_copy(src, dst, in_sem.at[n])
+        for n, (src, dst) in enumerate(
+            ((g_h, g_v), (win_h, win_v), (wo_h, wo_v), (blend_h, blend_v), (both_h, both_v))
+        )
+    ]
+    for copy in loads:
+        copy.start()
+    for copy in loads[:3]:
+        copy.wait()
+    for c in range(8):
+        g[2 * c : 2 * c + 2, :] = g_v[c]
+    w = win_v[...]
     w3 = jnp.concatenate([w, w, w], axis=0)
     mean = jnp.mean(w.astype(f32), axis=1, keepdims=True)
-    wot = wo[...]
+    wot = wo_v[...]
     wot3 = jnp.concatenate([wot, wot, wot], axis=0)
     half = D // 2
     copies = []
+
+    def put(src, dst):
+        copy = pltpu.make_async_copy(src, dst, out_sem.at[len(copies)])
+        copy.start()
+        copies.append(copy)
+
     for n, out in enumerate((gv_o, gg_o, gd_o)):
         rows = g[:, D * n : D * n + D]
         stack = jnp.concatenate(split3(rows), axis=0)
@@ -524,14 +546,16 @@
             if n < 2:
                 block = block - jnp.sum(mean * rows, axis=0, keepdims=True)
             out_s[n, half * h : half * h + half, :] = block
-            copy = pltpu.make_async_copy(
-                out_s.at[n, pl.ds(half * h, half)], out.at[pl.ds(half * h, half)], out_sem.at[2 * n + h]
-            )
-            copy.start()
-            copies.append(copy)
-    blend_o[...] = blend[...]
-    gin_o[...] = both[0:F, :]
-    gout_o[...] = both[F : 2 * F, :]
+            put(out_s.at[n, pl.ds(half * h, half)], out.at[pl.ds(half * h, half)])
+    for copy in loads[3:]:
+        copy.wait()
+    for q in range(MP):
+        blend_s[3 * q : 3 * q + 3, :] = blend_v[q]
+    for n in range(2 * F):
+        both_s[n : n + 1, :] = both_v[n]
+    put(blend_s, blend_o)
+    put(both_s.at[0:F], gin_o)
+    put(both_s.at[F : 2 * F], gout_o)
     for copy in copies:
         copy.wait()
 
@@ -539,7 +563,6 @@
 def per_device(latent, reward_grad, curvature, offsets, counts, w_in, w_value, w_gate, w_down, w_out):
     vm = pltpu.VMEM
     any_spec = pl.BlockSpec(memory_space=pl.ANY)
-    vm_spec = pl.BlockSpec(memory_space=pltpu.VMEM)
     tokens = 2 * HALF * HALF
     dma = pltpu.SemaphoreType.DMA
     scratch = [
@@ -554,15 +577,15 @@
         vm((8, 2, PAY), f32), vm((2 * F, D), f32), vm((2 * F, 1, D), f32), vm((2 * F, 1, D), f32), vm((8, 1, D), f32),
         vm((1, D), f32), vm((2 * F, 1, D), f32),
         vm((SLAB, COLS), bf16), vm((SLAB, CELLS), jnp.int32), pltpu.SemaphoreType.REGULAR((7,)), dma((2,)),
-        dma((9,)), dma((136,)), dma((2, 4)), dma((16,)), dma((16,)), dma((MP,)), dma((8,)), dma((8,)), dma((8,)),
+        dma((12,)), dma((136,)), dma((2, 4)), dma((16,)), dma((16,)), dma((MP,)), dma((8,)), dma((8,)), dma((8,)),
         dma((2 * F,)), dma((8,)), dma((2 * F,)),
     ]
     sds = jax.ShapeDtypeStruct
     blend, g, both = pl.pallas_call(
         main_kernel,
-        out_shape=(sds((SLAB, COLS), f32), sds((F, 3 * D), f32), sds((2 * F, D), f32)),
+        out_shape=(sds((MP, 3, COLS), f32), sds((8, 2, PAY), f32), sds((2 * F, 1, D), f32)),
         in_specs=[any_spec] * 9,
-        out_specs=(vm_spec,) * 3,
+        out_specs=(any_spec,) * 3,
         scratch_shapes=scratch,
         compiler_params=pltpu.CompilerParams(
             collective_id=0, has_side_effects=True, vmem_limit_bytes=56 * 1024 * 1024
@@ -575,9 +598,12 @@
             sds((SLAB, COLS), f32), sds((F, D), f32), sds((D, D), f32), sds((D, D), f32), sds((D, D), f32),
             sds((F, D), f32),
         ),
-        in_specs=[vm_spec] * 5,
-        out_specs=(vm_spec, vm_spec, any_spec, any_spec, any_spec, vm_spec),
-        scratch_shapes=[vm((3, D, D), f32), dma((6,))],
+        in_specs=[any_spec] * 5,
+        out_specs=(any_spec,) * 6,
+        scratch_shapes=[
+            vm((MP, 3, COLS), f32), vm((8, 2, PAY), f32), vm((2 * F, 1, D), f32), vm((F, D), bf16), vm((F, D), bf16),
+            vm((F, PAY), f32), vm((SLAB, COLS), f32), vm((2 * F, D), f32), vm((3, D, D), f32), dma((5,)), dma((9,)),
+        ],
         name="weight_outputs",
     )(blend, g, both, w_in, w_out.T)
     return (*outs, grad_out.T)

time: 52 us -> 50.6 us (0.973)
  Pallas kernels: 51.2 us -> 49.8 us
    pallas_call x1, Pallas kernels: 46.9 us -> 46.1 us  [per_device(): pl.pallas_call(main_kernel, out_shape=(sds((MP, 3, COLS), f32), sds((8, 2...]
    pallas_call x1, Pallas kernels: 4.34 us -> 3.69 us  [per_device(): pl.pallas_call(final_kernel, out_shape=(sds((SLAB, COLS), f32), sds((F, D...]
where the time goes in v3:
time: 50.6 us; the launch traced here: 50.4 us
  Pallas kernels  49.8 us (98%)
  between operations  0.64 us (1%)
    pallas_call x1, Pallas kernels, per_device(): pl.pallas_call(main_kernel, out_shape=(sds((MP, 3, COLS), f32), sds((8, 2...  46.1 us
    pallas_call x1, Pallas kernels, per_device(): pl.pallas_call(final_kernel, out_shape=(sds((SLAB, COLS), f32), sds((F, D...  3.69 us

profile of v3, /device:TPU:1, one launch (start us, length us, event | category | flops | bytes accessed | tf_op | source)
XLA Modules:
  0.0 50.4 jit_solution(13850056243784131537)
XLA Ops:
  0.6 46.1 %tile_gradients.1 = (f32[4,3,384]{2,1,0:T(4,128)}, f32[8,2,1920]{2,1,0:T(2,128)}, f32[32,1,640]{2,1,0:T(1,128)}) custom-call(bf16[12,384]{1,0:T(8,128)(2,1)} %lat_h.1, f32[12,384]{1,0:T(8,128)} %rew_h.1, f32[12,384]{1,0:T(8,128)} %cur_h.1, s32[12,96]{1,0:T(8,128)} %cnt_h.1, bf16[16,640]{1,0:T(8,128)(2,1)} %win_h.3, bf16[640,640]{1,0:T(8,128)(2,1)} %wv_h.1, ...), custom_call_target="tpu_custom_call" | custom-call | tf_op jit(solution)/shard_map/tile_gradients/pallas_call | solution.py:584
  46.7 3.7 %weight_outputs.1 = (f32[12,384]{1,0:T(8,128)}, f32[16,640]{1,0:T(8,128)}, f32[640,640]{1,0:T(8,128)}, f32[640,640]{1,0:T(8,128)}, f32[640,640]{1,0:T(8,128)}, /*index=5*/f32[16,640]{1,0:T(8,128)}) custom-call(f32[4,3,384]{2,1,0:T(4,128)} %get-tuple-element.15.blend_h, f32[8,2,1920]{2,1,0:T(2,128)} %get-tuple-element.16.g_h, ...), custom_call_target="tpu_custom_call" | custom-call | tf_op jit(solution)/shard_map/weight_outputs/pallas_call | solution.py:595

commit v4 on v3

--- a/solution.py
+++ b/solution.py
@@ -75,7 +75,7 @@
     regf, cntf, x_s, hid_s, gel_s, vs_s, q_s, act_s,
     part_s, rs_send, rs_in, cot_in, blend_in, cot_mine, blend_mine, wdo_s, woe_s, wrep_s,
     pay_s, pay_send, pay_in, z_in, z_mine, g_in, ps_s, ps_send, ps_in, pz_in, pz_mine, p_in,
-    lat_own, cnt_own, relay_sem, slab_sem,
+    lat_own, cnt_own, relay_sem, slab_sem, many_sem,
     loc_sem, send_sem, halo_sem, rs_sem, cot_sem, blend_sem, pay_sem, z_sem, g_sem, ps_sem, pz_sem, p_sem,
 ):
     t = lax.axis_index("tile")
@@ -161,10 +161,22 @@
             device_id=target, device_id_type=MESH,
         )
 
-    def send(src, dst, sem, target):
-        copy = remote(src, dst, len(sent), sem, target)
+    def send(src, dst, sem, target, group_sem=None):
+        if group_sem is None:
+            copy = remote(src, dst, len(sent), sem, target)
+            sent.append((None, copy))
+        else:
+            copy = pltpu.make_async_remote_copy(
+                src_ref=src, dst_ref=dst, send_sem=many_sem.at[group_sem], recv_sem=sem,
+                device_id=target, device_id_type=MESH,
+            )
         copy.start()
-        sent.append((None, copy))
+
+    def all_sent(ref, group_sem):
+        pltpu.make_async_remote_copy(
+            src_ref=ref, dst_ref=ref, send_sem=many_sem.at[group_sem], recv_sem=many_sem.at[group_sem],
+            device_id=(t, p), device_id_type=MESH,
+        ).wait_send()
 
     def send_if(cond, src, dst, sem, target):
         copy = remote(src, dst, len(sent), sem, target)
@@ -321,10 +333,10 @@
     hear(1)
     hear(5)
     for dev, q, kk in own_chip:
-        send(rs_send.at[4 + 4 * kk + q], rs_in.at[4 * k + p], rs_sem.at[4 * k + p], (dev, q))
+        send(rs_send.at[4 + 4 * kk + q], rs_in.at[4 * k + p], rs_sem.at[0], (dev, q), 0)
     for q in range(MP):
-        send(rs_send.at[q], rs_in.at[8 + 4 * k + p], rs_sem.at[8 + 4 * k + p], (2 * up_chip + 1, q))
-        send(rs_send.at[12 + q], rs_in.at[8 + 4 * k + p], rs_sem.at[8 + 4 * k + p], (2 * down_chip, q))
+        send(rs_send.at[q], rs_in.at[8 + 4 * k + p], rs_sem.at[0], (2 * up_chip + 1, q), 0)
+        send(rs_send.at[12 + q], rs_in.at[8 + 4 * k + p], rs_sem.at[0], (2 * down_chip, q), 0)
     rs_in[4 * k + p] = rs_send[4 + 4 * k + p]
 
     tell(2, along)
@@ -360,10 +372,7 @@
     rew3 = my_rows(rew)
     cur3 = my_rows(cur)
 
-    for dev, q, kk in own_chip:
-        arrive(rs_in.at[4 * kk + q], rs_sem.at[4 * kk + q])
-    for slot in range(8, 16):
-        arrive(rs_in.at[slot], rs_sem.at[slot])
+    arrive(rs_in.at[0:15], rs_sem.at[0])
     sums = []
     for kk in range(2):
         part = rs_in[4 * kk]
@@ -378,21 +387,17 @@
     cot_mine[0] = cot3[:, 0:WIN]
     cot_mine[1] = cot3[:, COLS - WIN : COLS]
     for dev, q, kk in own_chip:
-        send(cot_mine.at[kk], cot_in.at[4 + 4 * k + p], cot_sem.at[4 + 4 * k + p], (dev, q))
+        send(cot_mine.at[kk], cot_in.at[4 + 4 * k + p], cot_sem.at[0], (dev, q), 1)
     slot = 12 * (1 - k) + p
     for kk in range(2):
         for q in range(MP):
-            send(cot_mine.at[kk], cot_in.at[slot], cot_sem.at[slot], (2 * beside + kk, q))
+            send(cot_mine.at[kk], cot_in.at[slot], cot_sem.at[0], (2 * beside + kk, q), 1)
     hear(2)
     hear(6)
     tell(3, along)
     cot_in[4 + 4 * k + p] = cot_mine[k]
 
-    for dev, q, kk in own_chip:
-        arrive(cot_in.at[4 + 4 * kk + q], cot_sem.at[4 + 4 * kk + q])
-    for q in range(MP):
-        arrive(cot_in.at[q], cot_sem.at[q])
-        arrive(cot_in.at[12 + q], cot_sem.at[12 + q])
+    arrive(cot_in.at[0:15], cot_sem.at[0])
     hear(3)
     for dq in range(1, MP):
         send(blend_mine, blend_in.at[p], blend_sem.at[p], (2 * mirror + k, (p + dq) % MP))
@@ -423,7 +428,7 @@
         pay_send[c] = pay_s[2 * c : 2 * c + 2, :].astype(pay_send.dtype)
 
     for dev, c in group:
-        send(pay_send.at[c], pay_in.at[member], pay_sem.at[member], (dev, p))
+        send(pay_send.at[c], pay_in.at[member], pay_sem.at[0], (dev, p), 2)
     pay_in[member] = pay_send[member]
 
     def rows_dot(piece, right, dims=((1,), (0,))):
@@ -442,46 +447,42 @@
         ps_send[n] = ps_s[n : n + 1, :]
     mine = MP * member + p
     for dev, q, n in every:
-        send(ps_send.at[n], ps_in.at[mine], ps_sem.at[mine], (dev, q))
+        send(ps_send.at[n], ps_in.at[mine], ps_sem.at[0], (dev, q), 4)
     ps_in[mine] = ps_send[mine]
 
-    for dev, c in group:
-        arrive(pay_in.at[c], pay_sem.at[c])
+    arrive(pay_in.at[0:7], pay_sem.at[0])
     rows = pay_in[0].astype(f32)
     for c in range(1, 8):
         rows = rows + pay_in[c].astype(f32)
     z_mine[...] = rows.astype(z_mine.dtype)
     for dev, c in planes:
-        send(z_mine, z_in.at[plane], z_sem.at[plane], (dev, p))
+        send(z_mine, z_in.at[plane], z_sem.at[0], (dev, p), 3)
     z_in[plane] = z_mine[...]
 
-    for dev, q, n in every:
-        arrive(ps_in.at[n], ps_sem.at[n])
+    arrive(ps_in.at[0 : 2 * F - 1], ps_sem.at[0])
     row = ps_in[0]
     for n in range(1, 2 * F):
         row = row + ps_in[n]
     pz_mine[...] = row
     for dev, c in planes:
-        send(pz_mine, pz_in.at[plane], pz_sem.at[plane], (dev, p))
+        send(pz_mine, pz_in.at[plane], pz_sem.at[0], (dev, p), 5)
     pz_in[plane] = row
 
-    for dev, c in planes:
-        arrive(z_in.at[c], z_sem.at[c])
+    arrive(z_in.at[0:7], z_sem.at[0])
     rows = z_in[0].astype(f32)
     for c in range(1, 8):
         rows = rows + z_in[c].astype(f32)
     g_in[member] = rows
     for dev, c in group:
-        send(g_in.at[member], g_in.at[member], g_sem.at[member], (dev, p))
-
-    for dev, c in planes:
-        arrive(pz_in.at[c], pz_sem.at[c])
+        send(g_in.at[member], g_in.at[member], g_sem.at[0], (dev, p), 6)
+
+    arrive(pz_in.at[0:7], pz_sem.at[0])
     row = pz_in[0]
     for c in range(1, 8):
         row = row + pz_in[c]
     p_in[mine] = row
     for dev, q, n in every:
-        send(p_in.at[mine], p_in.at[mine], p_sem.at[mine], (dev, q))
+        send(p_in.at[mine], p_in.at[mine], p_sem.at[0], (dev, q), 7)
 
     for dq in range(1, MP):
         q = (p + dq) % MP
@@ -494,12 +495,15 @@
     outs = [(blend_in, blend_o), (g_in, g_o), (p_in, p_o)]
     outs = [pltpu.make_async_copy(src, dst, loc_sem.at[9 + n]) for n, (src, dst) in enumerate(outs)]
     outs[0].start()
-    for dev, c in group:
-        arrive(g_in.at[c], g_sem.at[c])
+    arrive(g_in.at[0:7], g_sem.at[0])
     outs[1].start()
-    for dev, q, n in every:
-        arrive(p_in.at[n], p_sem.at[n])
+    arrive(p_in.at[0 : 2 * F - 1], p_sem.at[0])
     outs[2].start()
+    for n, ref in enumerate((
+        rs_in.at[0:15], cot_in.at[0:15], pay_in.at[0:7], z_in.at[0:7], ps_in.at[0 : 2 * F - 1], pz_in.at[0:7],
+        g_in.at[0:7], p_in.at[0 : 2 * F - 1],
+    )):
+        all_sent(ref, n)
     for cond, copy in sent:
         if cond is None:
             copy.wait_send()
@@ -576,9 +580,9 @@
         vm((F, PAY), f32), vm((8, 2, PAY), LINK), vm((8, 2, PAY), LINK), vm((8, 2, PAY), LINK), vm((2, PAY), LINK),
         vm((8, 2, PAY), f32), vm((2 * F, D), f32), vm((2 * F, 1, D), f32), vm((2 * F, 1, D), f32), vm((8, 1, D), f32),
         vm((1, D), f32), vm((2 * F, 1, D), f32),
-        vm((SLAB, COLS), bf16), vm((SLAB, CELLS), jnp.int32), pltpu.SemaphoreType.REGULAR((7,)), dma((2,)),
-        dma((12,)), dma((136,)), dma((2, 4)), dma((16,)), dma((16,)), dma((MP,)), dma((8,)), dma((8,)), dma((8,)),
-        dma((2 * F,)), dma((8,)), dma((2 * F,)),
+        vm((SLAB, COLS), bf16), vm((SLAB, CELLS), jnp.int32), pltpu.SemaphoreType.REGULAR((7,)), dma((2,)), dma((8,)),
+        dma((12,)), dma((16,)), dma((2, 4)), dma((1,)), dma((1,)), dma((MP,)), dma((1,)), dma((1,)), dma((1,)),
+        dma((1,)), dma((1,)), dma((1,)),
     ]
     sds = jax.ShapeDtypeStruct
     blend, g, both = pl.pallas_call(

time: 50.6 us -> 48.4 us (0.957)
  Pallas kernels: 49.8 us -> 47.6 us
    pallas_call x1, Pallas kernels: 46.1 us -> 43.9 us  [per_device(): pl.pallas_call(main_kernel, out_shape=(sds((MP, 3, COLS), f32), sds((8, 2...]
where the time goes in v4:
time: 48.4 us; the launch traced here: 48.2 us
  Pallas kernels  47.6 us (98%)
  between operations  0.64 us (1%)
    pallas_call x1, Pallas kernels, per_device(): pl.pallas_call(main_kernel, out_shape=(sds((MP, 3, COLS), f32), sds((8, 2...  43.9 us
    pallas_call x1, Pallas kernels, per_device(): pl.pallas_call(final_kernel, out_shape=(sds((SLAB, COLS), f32), sds((F, D...  3.69 us

profile of v4, /device:TPU:1, one launch (start us, length us, event | category | flops | bytes accessed | tf_op | source)
XLA Modules:
  0.0 48.2 jit_solution(12155242080868516066)
XLA Ops:
  0.6 43.9 %tile_gradients.1 = (f32[4,3,384]{2,1,0:T(4,128)}, f32[8,2,1920]{2,1,0:T(2,128)}, f32[32,1,640]{2,1,0:T(1,128)}) custom-call(bf16[12,384]{1,0:T(8,128)(2,1)} %lat_h.1, f32[12,384]{1,0:T(8,128)} %rew_h.1, f32[12,384]{1,0:T(8,128)} %cur_h.1, s32[12,96]{1,0:T(8,128)} %cnt_h.1, bf16[16,640]{1,0:T(8,128)(2,1)} %win_h.3, bf16[640,640]{1,0:T(8,128)(2,1)} %wv_h.1, ...), custom_call_target="tpu_custom_call" | custom-call | tf_op jit(solution)/shard_map/tile_gradients/pallas_call | solution.py:588
  44.5 3.7 %weight_outputs.1 = (f32[12,384]{1,0:T(8,128)}, f32[16,640]{1,0:T(8,128)}, f32[640,640]{1,0:T(8,128)}, f32[640,640]{1,0:T(8,128)}, f32[640,640]{1,0:T(8,128)}, /*index=5*/f32[16,640]{1,0:T(8,128)}) custom-call(f32[4,3,384]{2,1,0:T(4,128)} %get-tuple-element.15.blend_h, f32[8,2,1920]{2,1,0:T(2,128)} %get-tuple-element.16.g_h, ...), custom_call_target="tpu_custom_call" | custom-call | tf_op jit(solution)/shard_map/weight_outputs/pallas_call | solution.py:599
